TPU v7x, 32 devices: a whole 2x2x4 slice. The times are simulated.
32 devices in a mesh: sec: 16 (over z, y, x), band: 2 (over core).
Axes of the slice: x: 2, y: 2, z: 4, core: 2. Of those that a mesh axis runs over, the one named last changes fastest.
Arguments:
- velocity: float32 [3, 32, 256, 512], P(None, 'band', 'sec'), may hold values from -6 to 6
- crop_level: int32 [16, 2, 16], P('sec', 'band'), may hold values from 0 to 12
- crop_x: int32 [16, 2, 16], P('sec', 'band'), may hold values from 0 to 4
- crop_y: int32 [16, 2, 16], P('sec', 'band'), may hold values from 0 to 248
- live_count: int32 [32], P(('sec', 'band')), may hold values from 1 to 16, 320 in all
- w_first: float32 [27, 64, 3], replicated, may hold values from -0.625 to 0.625
- norm_gain: float32 [64], replicated, may hold values from 0.25 to 1.75
- norm_shift: float32 [64], replicated, may hold values from -3 to 3
- w_middle: float32 [27, 64, 64], replicated, may hold values from -0.15625 to 0.15625
- w_last: float32 [27, 6, 64], replicated, may hold values from -0.15625 to 0.15625
Outputs:
- velocity_next: float32 [3, 32, 256, 512], P(None, 'band', 'sec')
- new_first: float32 [27, 64, 3], replicated
- new_gain: float32 [64], replicated
- new_shift: float32 [64], replicated
- new_middle: float32 [27, 64, 64], replicated
- new_last: float32 [27, 6, 64], replicated
- loss: float32 [], replicated
Inputs may be any that keep to these rules, and one draw needn't show every extreme that they name: `live_count`: the counts sum to 320.
All inputs are finite; a program needn't handle non-finite values. No bound on the sum of `live_count` on one device may be relied on, other than what follows from the above.
Results may differ from a plain program's by a relative error of at most 0.00043.
Values may be sent and summed in bfloat16 or wider, within the bound.
No kernel may reach another device: no remote copies, remote signals or barrier semaphores. Data moves between devices by JAX's collectives and lax.ppermute only.
A program may use at most 320 MiB of HBM per device.

v0:
```python
import functools

import jax
import jax.numpy as jnp
from jax import lax
from jax.experimental import pallas as pl
from jax.experimental.pallas import tpu as pltpu
from jax.sharding import PartitionSpec as P

PZ = 4
PX = 4
PY = 8
CH = 64
LANES = 128
KIN = PZ * PX
CHUNK = LANES // PY
FIELD_ROWS = 16
TAP_ROWS = 27 * 8

TIME_STEP = 0.2
VISCOSITY = 0.5
LEARNING = 1.0
EPSILON = 1e-05
PAIRS = ((0, 0), (1, 1), (2, 2), (0, 1), (0, 2), (1, 2))
OFFSETS = (-1, 0, 1)
TAPS = [(dz, dx, dy) for dz in OFFSETS for dx in OFFSETS for dy in OFFSETS]

F32 = jnp.float32
BF16 = jnp.bfloat16
VMEM = pl.BlockSpec(memory_space=pltpu.VMEM)
SMEM = pl.BlockSpec(memory_space=pltpu.SMEM)
ANY = pl.BlockSpec(memory_space=pl.ANY)
PARAMS = pltpu.CompilerParams(vmem_limit_bytes=60 * 1024 * 1024)

MID_TILES = 4
MID_ROWS = 3 * CH
HALF_BASE = MID_TILES * MID_ROWS
PLANE_BASE = HALF_BASE + MID_ROWS // 2
PLANE_STEP = 32
MISC_BASE = PLANE_BASE + 4 * PLANE_STEP + 27
EXCHANGE_ROWS = 1024


def nt(left, right):
    return lax.dot_general(left, right, (((1,), (1,)), ((), ())), preferred_element_type=F32)


def mm(left, right):
    return lax.dot_general(left, right, (((1,), (0,)), ((), ())), preferred_element_type=F32)


def tn(left, right):
    return lax.dot_general(left, right, (((0,), (0,)), ((), ())), preferred_element_type=F32)


def each(number, body):
    if number == 1:
        body(0)
    else:
        lax.fori_loop(0, number, lambda i, c: (body(i), c)[1], 0)


def weights_kernel(wf_ref, wm_ref, wl_ref, w1_ref, w2f_ref, w2b_ref, w3f_ref, w3b_ref, rows):
    rows[...] = jnp.zeros_like(rows)
    for c in range(3):
        rows[pl.ds(c, 27, stride=8), :] = wf_ref[c]
    w1_ref[...] = jnp.transpose(rows[...]).astype(BF16)
    rows[...] = jnp.zeros_like(rows)
    for o in range(6):
        rows[pl.ds(o, 27, stride=8), :] = wl_ref[o]
    w3f_ref[...] = rows[...].astype(BF16)
    w3b_ref[...] = jnp.transpose(rows[...]).astype(BF16)
    for z in range(3):
        taps = [wm_ref[z * 9 + j] for j in range(9)]
        w2f_ref[z * CH : (z + 1) * CH, :] = jnp.concatenate(taps, axis=1).astype(BF16)
        turned = jnp.transpose(jnp.concatenate(taps, axis=0))
        w2b_ref[z * CH : (z + 1) * CH, :] = turned.astype(BF16)


def arrange_weights(wf, wm, wl):
    return pl.pallas_call(
        weights_kernel,
        out_shape=(
            jax.ShapeDtypeStruct((CH, TAP_ROWS), BF16),
            jax.ShapeDtypeStruct((3 * CH, 9 * CH), BF16),
            jax.ShapeDtypeStruct((3 * CH, 9 * CH), BF16),
            jax.ShapeDtypeStruct((TAP_ROWS, CH), BF16),
            jax.ShapeDtypeStruct((CH, TAP_ROWS), BF16),
        ),
        in_specs=[VMEM] * 3,
        out_specs=(VMEM,) * 5,
        scratch_shapes=[pltpu.VMEM((TAP_ROWS, CH), F32)],
        name="arrange_weights",
    )(wf, wm, wl)


def lane_values(values_ref, base, lanes):
    which = (lanes % LANES) // PY
    out = jnp.zeros(lanes.shape, jnp.int32)
    for k in range(CHUNK):
        out = jnp.where(which == k, values_ref[base + k], out)
    return out


def flow_kernel(place_ref, level_ref, cx_ref, cy_ref, v_ref, a_ref, b_ref, c_ref, out_ref, crop_ref, vn, parts, chosen, sems):
    odd = place_ref[0] == 1
    upper_band = place_ref[1] == 1
    _, levels, nx, ny = v_ref.shape
    row = lax.broadcasted_iota(jnp.int32, (nx, ny), 0)
    copies = []
    for l in range(levels):
        centre = [v_ref[c, l] for c in range(3)]
        nxt = []
        for c in range(3):
            first = a_ref[c, l : l + 1, :]
            second = b_ref[c, l : l + 1, :]
            west = jnp.where(odd, first, second)
            east = jnp.where(odd, second, first)
            beyond = c_ref[c]
            if l + 1 < levels:
                upper = v_ref[c, l + 1]
            else:
                upper = jnp.where(upper_band, 0.0, beyond)
            if l > 0:
                lower = v_ref[c, l - 1]
            else:
                lower = jnp.where(upper_band, beyond, 0.0)
            mid = centre[c]
            eastern = jnp.where(row == nx - 1, east, pltpu.roll(mid, nx - 1, 0))
            western = jnp.where(row == 0, west, pltpu.roll(mid, 1, 0))
            northern = pltpu.roll(mid, ny - 1, 1)
            southern = pltpu.roll(mid, 1, 1)
            laplace = upper + lower + eastern + western + northern + southern - 6.0 * mid
            advect = (
                centre[0] * (eastern - western) * 0.5
                + centre[1] * (northern - southern) * 0.5
                + centre[2] * (upper - lower) * 0.5
            )
            new = mid + TIME_STEP * (VISCOSITY * laplace - advect)
            vn[c, l] = new
            nxt.append(new)
        copy = pltpu.make_async_copy(vn.at[:, l], out_ref.at[:, l], sems.at[l])
        copy.start()
        copies.append(copy)
        new = jnp.concatenate(nxt, axis=0)
        high = new.astype(BF16)
        rest = new - high.astype(F32)
        middle = rest.astype(BF16)
        low = (rest - middle.astype(F32)).astype(BF16)
        parts[l * 9 * nx : (l + 1) * 9 * nx, :] = jnp.concatenate([high, middle, low], axis=0)

    lanes = lax.broadcasted_iota(jnp.int32, (1, 2 * LANES), 1)
    position = lax.broadcasted_iota(jnp.int32, (ny, 2 * LANES), 0)
    ch_rows = 9 * PZ * 8
    r = lax.broadcasted_iota(jnp.int32, (ch_rows, KIN * FIELD_ROWS), 0)
    col = lax.broadcasted_iota(jnp.int32, (ch_rows, KIN * FIELD_ROWS), 1)
    channel = r >> 5
    slot = jnp.where(channel < 3, channel, channel + 5)
    goal = ((((r >> 3) & 3) * PX + ((r & 7) >> 1)) * FIELD_ROWS) + slot
    place = jnp.where((col == goal) & ((r & 1) == 0), 1.0, 0.0).astype(BF16)

    def chunk(k):
        base = k * CHUNK
        level_of = lane_values(level_ref, base, lanes)
        x_of = lane_values(cx_ref, base, lanes)
        y_of = lane_values(cy_ref, base, lanes)
        source = 2 * (y_of + lanes % PY) + lanes // LANES
        picks = jnp.where(position == source, 1.0, 0.0).astype(BF16)
        half = levels // 2
        for part in range(2):
            span = half * 9 * nx
            got = mm(parts[part * span : (part + 1) * span, :], picks)
            for i in range(half):
                at = i * 9 * nx
                w = 3 * nx
                chosen[part * half + i] = (got[at : at + w] + got[at + w : at + 2 * w]) + got[at + 2 * w : at + 3 * w]
        rows = [None] * (9 * PZ)
        for l in range(PZ):
            window = []
            for c in range(3):
                take = slice(c * nx, (c + 1) * nx)
                kept = chosen[l, take, :]
                for o in range(1, levels - PZ + 1):
                    kept = jnp.where(level_of == o, chosen[o + l, take, :], kept)
                cells = kept[0 : 2 * PX]
                for o in range(1, nx // 2 - PX + 1):
                    cells = jnp.where(x_of == o, kept[2 * o : 2 * o + 2 * PX], cells)
                window.append(cells)

            def box(cells):
                pair = cells[:, :LANES] + cells[:, LANES:]
                return (pair + pltpu.roll(pair, 2 * PX - 1, 0)) * 0.25

            means = [box(cells) for cells in window]
            for c in range(3):
                rows[c * PZ + l] = means[c]
            for n, (i, j) in enumerate(PAIRS):
                rows[(3 + n) * PZ + l] = box(window[i] * window[j]) - means[i] * means[j]
        fields = jnp.concatenate(rows, axis=0).astype(BF16)
        crop_ref[k] = tn(fields, place).astype(BF16)

    each(crop_ref.shape[0], chunk)
    for copy in copies:
        copy.wait()


def flow_step(place, level, cx, cy, velocity, first, second, beyond):
    chunks = level.shape[0] // CHUNK
    _, levels, nx, ny = velocity.shape
    return pl.pallas_call(
        flow_kernel,
        out_shape=(
            jax.ShapeDtypeStruct(velocity.shape, F32),
            jax.ShapeDtypeStruct((chunks, LANES, KIN * FIELD_ROWS), BF16),
        ),
        in_specs=[SMEM] * 4 + [VMEM] * 4,
        out_specs=(ANY, VMEM),
        scratch_shapes=[
            pltpu.VMEM(velocity.shape, F32),
            pltpu.VMEM((levels * 9 * nx, ny), BF16),
            pltpu.VMEM((levels, 3 * nx, 2 * LANES), F32),
            pltpu.SemaphoreType.DMA((levels,)),
        ],
        compiler_params=PARAMS,
        name="flow_step",
    )(place, level, cx, cy, velocity, first, second, beyond)


def train_kernel(
    factor, count_ref, batch_ref, gain_ref, shift_ref, w1_ref, w2f_ref, w2b_ref, w3f_ref, w3b_ref,
    out_ref, sx, hidden, s2, h2, act2, tap_out, des, dys, dn, flat, g2, small,
):
    chunks = batch_ref.shape[0]
    width = KIN * LANES
    band = PX * LANES
    count = count_ref[0]
    points = count.astype(F32) * (KIN * PY)
    lane = lax.broadcasted_iota(jnp.int32, (1, LANES), 1)
    y = lane % PY
    inside = {-1: y > 0, 1: y < PY - 1}

    def live(k):
        return jnp.where(k * CHUNK + lane // PY < count, 1.0, 0.0)

    def shifted(block, dy):
        if dy == 0:
            return block
        return jnp.where(inside[dy], pltpu.roll(block, (-dy) % LANES, 1), 0.0)

    def at(l, x):
        return slice((l * PX + x) * LANES, (l * PX + x + 1) * LANES)

    def stack_taps(blocks, sign, store):
        moved = {dy: [shifted(block, dy) for block in blocks] for dy in OFFSETS}
        zero = jnp.zeros((8, LANES), F32)
        for l in range(PZ):
            for x in range(PX):
                column = []
                for dz, dx, dy in TAPS:
                    lz, xx = l + sign * dz, x + sign * dx
                    ok = 0 <= lz < PZ and 0 <= xx < PX
                    column.append(moved[sign * dy][lz * PX + xx] if ok else zero)
                store(at(l, x), jnp.concatenate(column, axis=0).astype(BF16))

    def stack_planes(block_of, sign):
        zero = jnp.zeros((CH, LANES), BF16)
        for l in range(PZ):
            for x in range(PX):
                block = block_of(l, x)
                for i, dy in enumerate(OFFSETS):
                    piece = shifted(block, sign * dy).astype(BF16)
                    for j, dx in enumerate(OFFSETS):
                        goal = x - sign * dx
                        if 0 <= goal < PX:
                            s2[(j * 3 + i) * CH : (j * 3 + i + 1) * CH, at(l, goal)] = piece
            for i in range(3):
                for j, dx in enumerate(OFFSETS):
                    edge = {-1: 0, 1: PX - 1}.get(sign * dx)
                    if edge is not None:
                        s2[(j * 3 + i) * CH : (j * 3 + i + 1) * CH, at(l, edge)] = zero

    def plane_products(weights, sign, target):
        for l in range(PZ):
            got = mm(weights[...], s2[:, l * band : (l + 1) * band])
            for i, dz in enumerate(OFFSETS):
                goal = l - sign * dz
                if 0 <= goal < PZ:
                    piece = got[i * CH : (i + 1) * CH]
                    where = slice(goal * band, (goal + 1) * band)
                    fresh = l == max(0, goal - 1)
                    if fresh:
                        target[:, where] = piece
                    else:
                        target[:, where] += piece

    def column(row):
        eye = lax.broadcasted_iota(jnp.int32, (CH, CH), 0) == lax.broadcasted_iota(jnp.int32, (CH, CH), 1)
        return jnp.sum(jnp.where(eye, row, 0.0), axis=1, keepdims=True)

    def line(col):
        eye = lax.broadcasted_iota(jnp.int32, (CH, CH), 0) == lax.broadcasted_iota(jnp.int32, (CH, CH), 1)
        return jnp.sum(jnp.where(eye, col, 0.0), axis=0, keepdims=True)

    gain = column(gain_ref[...])
    shift = column(shift_ref[...])
    eye_rows = KIN * FIELD_ROWS
    eye = jnp.where(
        lax.broadcasted_iota(jnp.int32, (eye_rows, eye_rows), 0)
        == lax.broadcasted_iota(jnp.int32, (eye_rows, eye_rows), 1),
        1.0,
        0.0,
    ).astype(BF16)

    flat[:, 0:LANES] = jnp.zeros((CH, LANES), F32)

    def first_pass(k):
        turned = nt(eye, batch_ref[k])
        blocks = [turned[b * FIELD_ROWS : b * FIELD_ROWS + 8] for b in range(KIN)]

        def store(where, value):
            sx[k, :, where] = value

        stack_taps(blocks, 1, store)
        mask = live(k)
        total = flat[:, 0:LANES]
        for l in range(PZ):
            got = mm(w1_ref[...], sx[k, :, l * band : (l + 1) * band])
            hidden[k, :, l * band : (l + 1) * band] = got
            for x in range(PX):
                total = total + got[:, x * LANES : (x + 1) * LANES] * mask
        flat[:, 0:LANES] = total

    each(chunks, first_pass)
    average = jnp.sum(flat[:, 0:LANES], axis=1, keepdims=True) / points
    flat[:, 0:LANES] = jnp.zeros((CH, LANES), F32)

    def second_pass(k):
        mask = live(k)
        total = flat[:, 0:LANES]
        for b in range(KIN):
            where = slice(b * LANES, (b + 1) * LANES)
            centred = hidden[k, :, where] - average
            hidden[k, :, where] = centred
            total = total + centred * centred * mask
        flat[:, 0:LANES] = total

    each(chunks, second_pass)
    variance = jnp.sum(flat[:, 0:LANES], axis=1, keepdims=True) / points
    inverse = lax.rsqrt(variance + EPSILON)

    g2[...] = jnp.zeros_like(g2)
    small[...] = jnp.zeros_like(small)
    flat[:, 0 : 2 * LANES] = jnp.zeros((CH, 2 * LANES), F32)
    flat[0:8, 2 * LANES : 3 * LANES] = jnp.zeros((8, LANES), F32)

    def main_pass(k):
        mask = live(k)

        def act_first(l, x):
            normed = hidden[k, :, at(l, x)] * inverse * gain + shift
            return normed * jax.nn.sigmoid(normed)

        stack_planes(act_first, 1)
        plane_products(w2f_ref, 1, h2)
        for b in range(KIN):
            where = slice(b * LANES, (b + 1) * LANES)
            pre = h2[:, where]
            act2[:, where] = (pre * jax.nn.sigmoid(pre)).astype(BF16)
        for l in range(PZ):
            where = slice(l * band, (l + 1) * band)
            tap_out[:, where] = mm(w3f_ref[...], act2[:, where])
        turned = nt(eye, batch_ref[k])
        errors = []
        lost = flat[0:8, 2 * LANES : 3 * LANES]
        for l in range(PZ):
            for x in range(PX):
                sums = {}
                for t, (dz, dx, dy) in enumerate(TAPS):
                    lz, xx = l + dz, x + dx
                    if 0 <= lz < PZ and 0 <= xx < PX:
                        piece = tap_out[t * 8 : (t + 1) * 8, at(lz, xx)]
                        sums[dy] = sums[dy] + piece if dy in sums else piece
                output = sums[0] + shifted(sums[-1], -1) + shifted(sums[1], 1)
                b = l * PX + x
                error = (output - turned[b * FIELD_ROWS + 8 : b * FIELD_ROWS + 16]) * mask
                lost = lost + error * error
                errors.append(2.0 * factor * error)
        flat[0:8, 2 * LANES : 3 * LANES] = lost

        def store(where, value):
            des[:, where] = value

        stack_taps(errors, -1, store)
        small[:, 0:CH] += nt(des[...], act2[...])
        for l in range(PZ):
            got = mm(w3b_ref[...], des[:, l * band : (l + 1) * band])
            for x in range(PX):
                where = at(l, x)
                cot = got[:, x * LANES : (x + 1) * LANES].astype(BF16).astype(F32)
                pre = h2[:, where]
                sig = jax.nn.sigmoid(pre)
                h2[:, where] = cot * (sig * (1.0 + pre * (1.0 - sig)))
        zero = jnp.zeros((CH, band), BF16)
        for l in range(PZ):
            piece = h2[:, l * band : (l + 1) * band].astype(BF16)
            for i, dz in enumerate(OFFSETS):
                if 0 <= l + dz < PZ:
                    dys[i * CH : (i + 1) * CH, (l + dz) * band : (l + dz + 1) * band] = piece
        dys[0:CH, (PZ - 1) * band :] = zero
        dys[2 * CH :, 0:band] = zero
        g2[...] += nt(dys[...], s2[...])
        stack_planes(lambda l, x: h2[:, at(l, x)], -1)
        plane_products(w2b_ref, -1, act_cot)
        by_gain = flat[:, 0:LANES]
        by_shift = flat[:, LANES : 2 * LANES]
        for b in range(KIN):
            where = slice(b * LANES, (b + 1) * LANES)
            cot = act_cot[:, where].astype(BF16).astype(F32)
            normal = hidden[k, :, where] * inverse
            normed = normal * gain + shift
            sig = jax.nn.sigmoid(normed)
            d_normed = cot * (sig * (1.0 + normed * (1.0 - sig)))
            by_gain = by_gain + d_normed * normal
            by_shift = by_shift + d_normed
            dn[k, :, where] = d_normed
        flat[:, 0:LANES] = by_gain
        flat[:, LANES : 2 * LANES] = by_shift

    act_cot = tap_out.at[0:CH]
    each(chunks, main_pass)
    grad_gain = jnp.sum(flat[:, 0:LANES], axis=1, keepdims=True)
    grad_shift = jnp.sum(flat[:, LANES : 2 * LANES], axis=1, keepdims=True)
    loss = jnp.sum(flat[0:8, 2 * LANES : 3 * LANES]) * factor

    from_mean = -inverse * (gain * grad_shift) / points
    from_variance = -(gain * grad_gain) * inverse * inverse / points
    scale = gain * inverse

    out_ref[...] = jnp.zeros_like(out_ref)

    def last_pass(k):
        mask = live(k)
        for b in range(KIN):
            where = slice(b * LANES, (b + 1) * LANES)
            d_hidden = dn[k, :, where] * scale + mask * (from_mean + from_variance * hidden[k, :, where])
            act2[:, where] = d_hidden.astype(BF16)
        small[:, CH:LANES] += nt(sx[k], act2[...])

    each(chunks, last_pass)

    for j in range(MID_TILES):
        out_ref[j * MID_ROWS : (j + 1) * MID_ROWS, :] = g2[:, j * LANES : (j + 1) * LANES]
    half = MID_ROWS // 2
    out_ref[HALF_BASE : HALF_BASE + half, 0:CH] = g2[0:half, MID_TILES * LANES :]
    out_ref[HALF_BASE : HALF_BASE + half, CH:LANES] = g2[half:, MID_TILES * LANES :]
    both = [small[pl.ds(o, 27, stride=8), :] for o in range(6)]
    planes = [pair[:, 0:CH] for pair in both] + [pair[:, CH:LANES] for pair in both[0:3]]
    for n, plane in enumerate(planes):
        base = PLANE_BASE + (n // 2) * PLANE_STEP
        side = (n % 2) * CH
        out_ref[base : base + 27, side : side + CH] = plane
    out_ref[MISC_BASE : MISC_BASE + 1, 0:CH] = line(grad_gain)
    out_ref[MISC_BASE : MISC_BASE + 1, CH:LANES] = line(grad_shift)
    out_ref[MISC_BASE + 1 : MISC_BASE + 2, :] = jnp.full((1, LANES), loss, F32)


def train(factor, count, batch, gain, shift, weights):
    chunks = batch.shape[0]
    width = KIN * LANES
    return pl.pallas_call(
        functools.partial(train_kernel, factor),
        out_shape=jax.ShapeDtypeStruct((EXCHANGE_ROWS, LANES), F32),
        in_specs=[SMEM] + [VMEM] * 8,
        out_specs=VMEM,
        scratch_shapes=[
            pltpu.VMEM((chunks, TAP_ROWS, width), BF16),
            pltpu.VMEM((chunks, CH, width), F32),
            pltpu.VMEM((9 * CH, width), BF16),
            pltpu.VMEM((CH, width), F32),
            pltpu.VMEM((CH, width), BF16),
            pltpu.VMEM((TAP_ROWS, width), F32),
            pltpu.VMEM((TAP_ROWS, width), BF16),
            pltpu.VMEM((3 * CH, width), BF16),
            pltpu.VMEM((chunks, CH, width), F32),
            pltpu.VMEM((CH, 3 * LANES), F32),
            pltpu.VMEM((3 * CH, 9 * CH), F32),
            pltpu.VMEM((TAP_ROWS, LANES), F32),
        ],
        compiler_params=PARAMS,
        name="train_step",
    )(count, batch, gain, shift, *weights)


def update_kernel(grad_ref, wf_ref, gain_ref, shift_ref, wm_ref, wl_ref, nf_ref, ng_ref, ns_ref, nm_ref, nl_ref):
    half = MID_ROWS // 2
    for z in range(3):
        for j in range(MID_TILES):
            block = grad_ref[j * MID_ROWS + z * CH : j * MID_ROWS + (z + 1) * CH, :]
            t = z * 9 + 2 * j
            nm_ref[t] = wm_ref[t] - LEARNING * block[:, :CH]
            nm_ref[t + 1] = wm_ref[t + 1] - LEARNING * block[:, CH:]
    fold = grad_ref[HALF_BASE : HALF_BASE + half, :]
    last = jnp.concatenate([fold[:, :CH], fold[:, CH:]], axis=0)
    for z in range(3):
        t = z * 9 + 8
        nm_ref[t] = wm_ref[t] - LEARNING * last[z * CH : (z + 1) * CH]
    for n in range(9):
        base = PLANE_BASE + (n // 2) * PLANE_STEP
        side = (n % 2) * CH
        plane = grad_ref[base : base + 27, side : side + CH]
        if n < 6:
            nl_ref[n] = wl_ref[n] - LEARNING * plane
        else:
            nf_ref[n - 6] = wf_ref[n - 6] - LEARNING * plane
    misc = grad_ref[MISC_BASE : MISC_BASE + 1, :]
    ng_ref[...] = gain_ref[...] - LEARNING * misc[:, :CH]
    ns_ref[...] = shift_ref[...] - LEARNING * misc[:, CH:]


def update(grads, wf, gain, shift, wm, wl):
    shapes = [wf, gain, shift, wm, wl]
    return pl.pallas_call(
        update_kernel,
        out_shape=tuple(jax.ShapeDtypeStruct(w.shape, F32) for w in shapes),
        in_specs=[VMEM] * 6,
        out_specs=(VMEM,) * 5,
        name="update",
    )(grads, *shapes)


def total(parts, axes):
    devices = lax.axis_size(axes)
    rows = parts.reshape(devices, EXCHANGE_ROWS // devices, LANES)
    mine = lax.all_to_all(rows, axes, split_axis=0, concat_axis=0, tiled=True)
    mine = jnp.sum(mine, axis=0)
    spread = jnp.broadcast_to(mine[None], rows.shape)
    whole = lax.all_to_all(spread, axes, split_axis=0, concat_axis=0, tiled=True)
    return whole.reshape(EXCHANGE_ROWS, LANES)


def on_device(
    velocity, crop_level, crop_x, crop_y, live_count, w_first, norm_gain, norm_shift, w_middle, w_last
):
    sources = lax.axis_size("sec")
    bands = lax.axis_size("band")
    assert bands == 2 and sources % 2 == 0
    groups = sources * bands
    sec = lax.axis_index("sec")
    odd = sec % 2
    band = lax.axis_index("band")
    place = jnp.stack([odd, band]).astype(jnp.int32)

    wf = jnp.transpose(w_first, (2, 0, 1))
    wl = jnp.transpose(w_last, (1, 0, 2))
    weights = arrange_weights(wf, w_middle, wl)

    head, tail = velocity[:, :, 0, :], velocity[:, :, -1, :]
    near = jnp.where(odd == 1, head, tail)
    far = jnp.where(odd == 1, tail, head)
    plane = jnp.where(band == 0, velocity[:, -1], velocity[:, 0])
    first = lax.ppermute(near, "sec", [(i, i ^ 1) for i in range(sources)])
    second = lax.ppermute(far, "sec", [(i, ((i + 1) ^ 1) - 1) for i in range(1, sources - 1)])
    beyond = lax.ppermute(plane, "band", [(0, 1), (1, 0)])

    velocity_next, crops = flow_step(
        place, crop_level.reshape(-1), crop_x.reshape(-1), crop_y.reshape(-1), velocity, first, second, beyond
    )
    crops = crops.reshape(sources, PY, KIN * FIELD_ROWS)
    batch = lax.all_to_all(crops, "sec", split_axis=0, concat_axis=0, tiled=True)
    batch = batch.reshape(sources // CHUNK, LANES, KIN * FIELD_ROWS)
    factor = 1.0 / (6.0 * PZ * PX * PY * (groups * sources * 5 // 8))
    gain, shift = norm_gain.reshape(1, CH), norm_shift.reshape(1, CH)
    parts = train(factor, live_count, batch, gain, shift, weights)
    grads = total(parts, ("sec", "band"))
    nf, ng, ns, nm, nl = update(grads, wf, gain, shift, w_middle, wl)
    return (
        velocity_next,
        jnp.transpose(nf, (1, 2, 0)),
        ng.reshape(CH),
        ns.reshape(CH),
        nm,
        jnp.transpose(nl, (1, 0, 2)),
        grads[MISC_BASE + 1, 0],
    )


def solution(mesh):
    in_specs = (
        P(None, "band", "sec", None),
        P("sec", "band", None),
        P("sec", "band", None),
        P("sec", "band", None),
        P(("sec", "band")),
        P(),
        P(),
        P(),
        P(),
        P(),
    )
    out_specs = (P(None, "band", "sec", None), P(), P(), P(), P(), P(), P())
    return jax.shard_map(
        on_device, mesh=mesh, in_specs=in_specs, out_specs=out_specs, check_vma=False
    )
```

profile of v0, /device:TPU:0, one launch (start us, length us, event | category | flops | bytes accessed | tf_op | source)
XLA Modules:
  0.0 80.4 jit_solution(5472077735268339549)
XLA Ops:
  0.6 1.6 %fusion.1 = (f32[3,16,1,512]{3,2,1,0:T(1,128)S(1)}, f32[3,16,1,512]{3,2,1,0:T(1,128)S(1)}) fusion(f32[3,16,16,512]{3,2,1,0:T(8,128)} %v_ref.1), kind=kLoop, calls=%fused_computation.5 | loop fusion | bytes 393216 | tf_op jit(solution)/shard_map/slice | solution.py:557
  2.2 3.0 %collective-permute-start = (f32[3,16,512]{2,1,0:T(8,128)S(1)}, f32[3,16,512]{2,1,0:T(8,128)S(1)}, u32[]{:S(2)}, u32[]{:S(2)}) collective-permute-start(f32[3,16,512]{2,1,0:T(8,128)S(1)} %get-tuple-element.34), channel_id=1, source_target_pairs={{0,2},{2,0},{4,6},{6,4},{8,10},{10,8},{12,14},{14,12},{16,18},{18,... | collective-permute-start | bytes 294920 | tf_op jit(solution)/shard_map/ppermute | solution.py:561
  5.3 0.7 collective-permute-start.1
  5.9 1.0 %fusion = f32[3,16,512]{2,1,0:T(8,128)S(1)} fusion(f32[3,16,16,512]{3,2,1,0:T(8,128)} %v_ref.1, pred[]{:T(512)S(6)} %eq.10), kind=kLoop, calls=%fused_computation.1 | loop fusion | flops 24576 | bytes 294913 | tf_op jit(solution)/shard_map/jit(_where)/select_n | solution.py:560
  6.9 0.1 collective-permute-start.2
  7.0 0.6 pad_add_fusion.place_ref
  7.6 0.5 collective-permute-done.a_ref
  8.1 0.0 copy-start.1
  8.1 0.0 collective-permute-done.1.b_ref
  8.1 0.0 copy-start.2
  8.1 0.2 collective-permute-done.2.c_ref
  8.3 0.0 copy-start.3
  8.3 0.4 copy-done.1
  8.7 0.0 copy-done.2
  8.7 0.2 copy-done.3
  8.9 5.0 %flow_step.1 = (f32[3,16,16,512]{3,2,1,0:T(8,128)}, bf16[1,128,256]{2,1,0:T(8,128)(2,1)}) custom-call(s32[2]{0:T(128)} %pad_add_fusion.place_ref, s32[16]{0:T(128)} %bitcast.43, s32[16]{0:T(128)} %bitcast.44, s32[16]{0:T(128)} %bitcast.45, f32[3,16,16,512]{3,2,1,0:T(8,128)} %v_ref.1, f32[3,16,512]{2,1,0:T(8,128)} %copy-done.1, f32[3,16,512]{2,1,0:T(8,128)} %copy-done.2, ...), custom_call_target="tpu_custom_call" | custom-call | tf_op jit(solution)/shard_map/flow_step/pallas_call | solution.py:210
  13.9 10.4 %all-to-all-start = ((bf16[16,8,256]{2,1,0:T(8,128)(2,1)}), bf16[16,8,256]{2,1,0:T(8,128)(2,1)S(1)}, u32[]{:S(2)}, u32[]{:S(2)}) async-start(bf16[16,8,256]{2,1,0:T(8,128)(2,1)} %bitcast.38), calls=%async_computation | async-start | bytes 131072 | tf_op jit(solution)/shard_map/all_to_all | solution.py:569
  24.9 2.2 %arrange_weights.1 = (bf16[64,216]{1,0:T(8,128)(2,1)}, bf16[192,576]{1,0:T(8,128)(2,1)}, bf16[192,576]{1,0:T(8,128)(2,1)}, bf16[216,64]{1,0:T(8,128)(2,1)}, bf16[64,216]{1,0:T(8,128)(2,1)}) custom-call(f32[3,27,64]{2,1,0:T(8,128)} %bitcast.36, f32[27,64,64]{2,1,0:T(8,128)} %wm_ref.3, f32[6,27,64]{2,1,0:T(8,128)} %bitcast.33), custom_call_target="tpu_custom_call" | custom-call | tf_op jit(solution)/shard_map/arrange_weights/pallas_call | solution.py:81
  27.1 4.7 %all-to-all-done = bf16[16,8,256]{2,1,0:T(8,128)(2,1)S(1)} async-done(((bf16[16,8,256]{2,1,0:T(8,128)(2,1)}), bf16[16,8,256]{2,1,0:T(8,128)(2,1)S(1)}, u32[]{:S(2)}, u32[]{:S(2)}) %all-to-all-start) | async-done | bytes 65568 | tf_op jit(solution)/shard_map/all_to_all | solution.py:569
  31.8 0.0 copy-start
  31.8 0.6 copy-done
  32.4 7.5 %train_step.1 = f32[1024,128]{1,0:T(8,128)} custom-call(s32[1]{0:T(128)S(6)} %copy.29.count_ref, bf16[1,128,256]{2,1,0:T(8,128)(2,1)} %bitcast.35, f32[1,64]{1,0:T(1,128)} %bitcast.39, f32[1,64]{1,0:T(1,128)} %bitcast.41, bf16[64,216]{1,0:T(8,128)(2,1)} %get-tuple-element.21.w1_ref, bf16[192,576]{1,0:T(8,128)(2,1)} %get-tuple-element.22.w2f_ref, ...), custom_call_target="tpu_custom_call" | custom-call | tf_op jit(solution)/shard_map/train_step/pallas_call | solution.py:470
  39.9 18.2 %all_to_all.15 = f32[32,32,128]{2,1,0:T(8,128)S(1)} all-to-all(f32[32,32,128]{2,1,0:T(8,128)} %bitcast.30), channel_id=1, replica_groups=mesh['sec'=16,'band'=2] {'sec','band'}, dimensions={0} | all-to-all | bytes 1048576 | tf_op jit(solution)/shard_map/all_to_all | solution.py:534
  58.2 0.1 broadcast_in_dim.2
  58.2 18.4 %all_to_all.16 = f32[32,32,128]{2,1,0:T(8,128)} all-to-all(f32[32,32,128]{2,1,0:T(8,128)S(1)} %broadcast_in_dim.2), channel_id=1, replica_groups=mesh['sec'=16,'band'=2] {'sec','band'}, dimensions={0} | all-to-all | bytes 1048576 | tf_op jit(solution)/shard_map/all_to_all | solution.py:537
  76.7 2.5 %update.1 = (f32[3,27,64]{2,1,0:T(8,128)}, f32[1,64]{1,0:T(1,128)}, f32[1,64]{1,0:T(1,128)}, f32[27,64,64]{2,1,0:T(8,128)}, f32[6,27,64]{2,1,0:T(8,128)}) custom-call(f32[1024,128]{1,0:T(8,128)} %bitcast.31, f32[3,27,64]{2,1,0:T(8,128)} %bitcast.37, f32[1,64]{1,0:T(1,128)} %bitcast.40, f32[1,64]{1,0:T(1,128)} %bitcast.42, f32[27,64,64]{2,1,0:T(8,128)} %wm_ref.3, ...), custom_call_target="tpu_custom_call" | custom-call | tf_op jit(solution)/shard_map/update/pallas_call | solution.py:522
  79.2 1.2 %slice.20 = f32[1,1]{1,0:T(1,128)} slice(f32[1024,128]{1,0:T(8,128)} %bitcast.32), slice={[1020:1021], [0:1]} | slice | bytes 8 | tf_op jit(solution)/shard_map/slice | solution.py:583
  (2 shorter events, 0.1 us)
Async XLA Ops:
  2.2 5.8 %collective-permute-start = (f32[3,16,512]{2,1,0:T(8,128)S(1)}, f32[3,16,512]{2,1,0:T(8,128)S(1)}, u32[]{:S(2)}, u32[]{:S(2)}) collective-permute-start(f32[3,16,512]{2,1,0:T(8,128)S(1)} %get-tuple-element.34), channel_id=1, source_target_pairs={{0,2},{2,0},{4,6},{6,4},{8,10},{10,8},{12,14},{14,12},{16,18},{18,... | collective-permute-start | bytes 294920 | tf_op jit(solution)/shard_map/ppermute | solution.py:561
  5.3 2.8 %collective-permute-start.1 = (f32[3,16,512]{2,1,0:T(8,128)S(1)}, f32[3,16,512]{2,1,0:T(8,128)S(1)}, u32[]{:S(2)}, u32[]{:S(2)}) collective-permute-start(f32[3,16,512]{2,1,0:T(8,128)S(1)} %get-tuple-element.33), channel_id=1, source_target_pairs={{2,4},{4,2},{6,8},{8,6},{10,12},{12,10},{14,16},{16,14},{18,20},{2... | collective-permute-start | bytes 294920 | tf_op jit(solution)/shard_map/ppermute | solution.py:562
  6.9 1.4 %collective-permute-start.2 = (f32[3,16,512]{2,1,0:T(8,128)S(1)}, f32[3,16,512]{2,1,0:T(8,128)S(1)}, u32[]{:S(2)}, u32[]{:S(2)}) collective-permute-start(f32[3,16,512]{2,1,0:T(8,128)S(1)} %fusion), channel_id=1, source_target_pairs={{0,1},{1,0},{2,3},{3,2},{4,5},{5,4},{6,7},{7,6},{8,9},{9,8},{10,11... | collective-permute-start | bytes 294920 | tf_op jit(solution)/shard_map/ppermute | solution.py:563
  8.1 0.6 copy-start.1
  8.1 0.7 copy-start.2
  8.3 0.6 copy-start.3
  13.9 17.9 %all-to-all-start = ((bf16[16,8,256]{2,1,0:T(8,128)(2,1)}), bf16[16,8,256]{2,1,0:T(8,128)(2,1)S(1)}, u32[]{:S(2)}, u32[]{:S(2)}) async-start(bf16[16,8,256]{2,1,0:T(8,128)(2,1)} %bitcast.38), calls=%async_computation | async-start | bytes 131072 | tf_op jit(solution)/shard_map/all_to_all | solution.py:569
  31.8 0.6 copy-start
where the time goes:
time: 80.8 us; the launch traced here: 80.4 us
  blocking collectives  36.6 us (45%)
  Pallas kernels  17.2 us (21%)
  starting transfers between devices  14.1 us (17%)
  waiting for transfers between devices  5.4 us (7%)
  local copies, waits for them, and re-layouts  4.06 us (5%)
  other arithmetic  1.62 us (2%)
  between operations  1.37 us (2%)
    all_to_all x1, blocking collectives, total(): lax.all_to_all(spread, axes, split_axis=0, concat_axis=0, tiled=True)  18.4 us
    all_to_all x1, blocking collectives, total(): mine = lax.all_to_all(rows, axes, split_axis=0, concat_axis=0, tiled=True)  18.2 us
    all_to_all x1, starting transfers between devices, on_device(): lax.all_to_all(crops, 'sec', split_axis=0, concat_axis=0, tiled=True)  10.4 us
    pallas_call x1, Pallas kernels, train(): pl.pallas_call(functools.partial(train_kernel, factor), out_shape=jax.Sha...  7.5 us
    pallas_call x1, Pallas kernels, flow_step(): pl.pallas_call(flow_kernel, out_shape=(jax.ShapeDtypeStruct(velocity.shap...  4.96 us
    all_to_all x1, waiting for transfers between devices, on_device(): lax.all_to_all(crops, 'sec', split_axis=0, concat_axis=0, tiled=True)  4.71 us
    ppermute x1, starting transfers between devices, on_device(): first = lax.ppermute(near, 'sec', [(i, i ^ 1) for i in range(sources)])  3.03 us
    pallas_call x1, Pallas kernels, update(): pl.pallas_call(update_kernel, out_shape=tuple((jax.ShapeDtypeStruct(w.sha...  2.52 us
  transfers between devices with their start and end apart: 4, of which 3 were waited for; matrix products, arithmetic and copies ran while one was open for 2% of the time, Pallas kernels for 3%

commit v1 on v0

v1 whole, which is shorter than its diff:
```python
import functools

import jax
import jax.numpy as jnp
from jax import lax
from jax.experimental import pallas as pl
from jax.experimental.pallas import tpu as pltpu
from jax.sharding import PartitionSpec as P

PZ = 4
PX = 4
PY = 8
CH = 64
LANES = 128
KIN = PZ * PX
CHUNK = LANES // PY
FIELD_ROWS = 16
TAP_ROWS = 27 * 8

TIME_STEP = 0.2
VISCOSITY = 0.5
LEARNING = 1.0
EPSILON = 1e-05
PAIRS = ((0, 0), (1, 1), (2, 2), (0, 1), (0, 2), (1, 2))
OFFSETS = (-1, 0, 1)
TAPS = [(dz, dx, dy) for dz in OFFSETS for dx in OFFSETS for dy in OFFSETS]

F32 = jnp.float32
BF16 = jnp.bfloat16
VMEM = pl.BlockSpec(memory_space=pltpu.VMEM)
SMEM = pl.BlockSpec(memory_space=pltpu.SMEM)
HBM = pl.BlockSpec(memory_space=pltpu.HBM)


def small_params(mib):
    return pltpu.CompilerParams(vmem_limit_bytes=min(mib, 60) * 1024 * 1024)


MID_ROWS = 9 * CH
HALF_BASE = MID_ROWS
PLANE_BASE = HALF_BASE + MID_ROWS // 2
PLANE_STEP = 32
PLANE_ROWS = 5 * PLANE_STEP
MISC_BASE = PLANE_BASE + 4 * PLANE_STEP + 27


def nt(left, right):
    return lax.dot_general(left, right, (((1,), (1,)), ((), ())), preferred_element_type=F32)


def mm(left, right):
    return lax.dot_general(left, right, (((1,), (0,)), ((), ())), preferred_element_type=F32)


def tn(left, right):
    return lax.dot_general(left, right, (((0,), (0,)), ((), ())), preferred_element_type=F32)


def shares(devices):
    mid, rest = -(-PLANE_BASE // devices), -(-PLANE_ROWS // devices)
    top = -(-(mid + rest) // 8) * 8
    return mid, rest, top, top + -(-rest // 8) * 8


def padded_rows(devices):
    mid, rest, _, _ = shares(devices)
    return devices * mid, max(PLANE_BASE + PLANE_ROWS, devices * mid, PLANE_BASE + devices * rest)


def two_parts(value):
    high = value.astype(BF16)
    return high, (value - high.astype(F32)).astype(BF16)


def fill(value, rows):
    missing = rows - value.shape[0]
    return jnp.concatenate([value, jnp.zeros((missing, LANES), F32)], axis=0) if missing else value


def each(number, body):
    if number == 1:
        body(0)
    else:
        lax.fori_loop(0, number, lambda i, c: (body(i), c)[1], 0)


def weights_kernel(wf_ref, wm_ref, wl_ref, w1_ref, w2f_ref, w2b_ref, w3f_ref, w3b_ref, rows):
    rows[...] = jnp.zeros_like(rows)
    for c in range(3):
        rows[pl.ds(c, 27, stride=8), :] = wf_ref[c]
    w1_ref[...] = jnp.transpose(rows[...]).astype(BF16)
    rows[...] = jnp.zeros_like(rows)
    for o in range(6):
        rows[pl.ds(o, 27, stride=8), :] = wl_ref[o]
    w3f_ref[...] = rows[...].astype(BF16)
    w3b_ref[...] = jnp.transpose(rows[...]).astype(BF16)
    for zx in range(9):
        taps = [wm_ref[zx * 3 + i] for i in range(3)]
        rows_at = slice(zx * CH, (zx + 1) * CH)
        w2f_ref[rows_at, :] = jnp.concatenate(taps, axis=1).astype(BF16)
        w2b_ref[rows_at, :] = jnp.transpose(jnp.concatenate(taps, axis=0)).astype(BF16)


def arrange_weights(wf, wm, wl):
    return pl.pallas_call(
        weights_kernel,
        out_shape=(
            jax.ShapeDtypeStruct((CH, TAP_ROWS), BF16),
            jax.ShapeDtypeStruct((9 * CH, 3 * CH), BF16),
            jax.ShapeDtypeStruct((9 * CH, 3 * CH), BF16),
            jax.ShapeDtypeStruct((TAP_ROWS, CH), BF16),
            jax.ShapeDtypeStruct((CH, TAP_ROWS), BF16),
        ),
        in_specs=[VMEM] * 3,
        out_specs=(VMEM,) * 5,
        scratch_shapes=[pltpu.VMEM((TAP_ROWS, CH), F32)],
        compiler_params=small_params(6),
        name="arrange_weights",
    )(wf, wm, wl)


def lane_values(values_ref, which_row, base, lanes):
    which = (lanes % LANES) // PY
    out = jnp.zeros(lanes.shape, jnp.int32)
    for k in range(CHUNK):
        out = jnp.where(which == k, values_ref[which_row, 0, base + k], out)
    return out


def fold_parts(got, rows):
    return (got[0:rows] + got[rows : 2 * rows]) + got[2 * rows : 3 * rows]


def shift_down(items, offset, wanted):
    step = 1 << (len(items) - wanted).bit_length()
    while step > 1:
        step //= 2
        keep = min(len(items), wanted + step - 1)
        chosen = (offset & step) != 0
        items = [
            jnp.where(chosen, items[i + step], items[i]) if i + step < len(items) else items[i] for i in range(keep)
        ]
    return items


def x_window(cells, x_of):
    kept = cells[0 : 2 * PX]
    for o in range(1, cells.shape[0] // 2 - PX + 1):
        kept = jnp.where(x_of == o, cells[2 * o : 2 * o + 2 * PX], kept)
    return kept


def three_parts(value):
    high = value.astype(BF16)
    rest = value - high.astype(F32)
    middle = rest.astype(BF16)
    low = (rest - middle.astype(F32)).astype(BF16)
    return jnp.concatenate([high, middle, low], axis=0)


def edges_kernel(source_ref, v_ref, near_ref, far_ref, plane_ref, loads):
    odd = lax.axis_index("sec") % 2 == 1
    upper_band = lax.axis_index("band") == 1
    _, levels, nx, ny = v_ref.shape
    arrivals = [
        pltpu.make_async_copy(source_ref.at[:, l], v_ref.at[:, l], loads.at[l]) for l in range(levels)
    ]
    for arrival in arrivals:
        arrival.start()
    for arrival in arrivals:
        arrival.wait()
    for c in range(3):
        head = v_ref[c, :, 0, :]
        tail = v_ref[c, :, nx - 1, :]
        near_ref[c] = jnp.where(odd, head, tail)
        far_ref[c] = jnp.where(odd, tail, head)
        plane_ref[c] = jnp.where(upper_band, v_ref[c, 0], v_ref[c, levels - 1])


def in_hbm(array):
    return pltpu.with_memory_space_constraint(array, pltpu.HBM)


def edges_step(velocity):
    _, levels, nx, ny = velocity.shape
    side = jax.ShapeDtypeStruct((3, levels, ny), F32)
    return pl.pallas_call(
        edges_kernel,
        out_shape=(
            jax.ShapeDtypeStruct(velocity.shape, F32), side, side, jax.ShapeDtypeStruct((3, nx, ny), F32)
        ),
        in_specs=[HBM],
        out_specs=(VMEM,) * 4,
        scratch_shapes=[pltpu.SemaphoreType.DMA((levels,))],
        compiler_params=small_params(6),
        cost_estimate=cost(10**6, 3 * 10**6),
        name="edges_step",
    )(in_hbm(velocity))


def inner_kernel(
    level_ref, cx_ref, cy_ref, v_ref, vn_ref, cells_ref, picks_ref, goal_ref, where_ref, parts, chosen, spots, sems
):
    _, levels, nx, ny = v_ref.shape
    chunks = cells_ref.shape[0]
    arrivals = [
        pltpu.make_async_copy(ref, spots.at[n], sems.at[n]) for n, ref in enumerate((level_ref, cx_ref, cy_ref))
    ]
    for arrival in arrivals:
        arrival.start()
    row = lax.broadcasted_iota(jnp.int32, (nx, ny), 0)
    share, slope = TIME_STEP * VISCOSITY, TIME_STEP * 0.5
    for l in range(levels):
        centre = [v_ref[c, l] for c in range(3)]
        u, v, w = [slope * field for field in centre]
        to_east = jnp.where(row == nx - 1, 0.0, share - u)
        to_west = jnp.where(row == 0, 0.0, share + u)
        to_north, to_south = share - v, share + v
        to_upper, to_lower = share - w, share + w
        nxt = []
        for c in range(3):
            mid = centre[c]
            new = (1.0 - 6.0 * share) * mid
            new = new + to_east * pltpu.roll(mid, nx - 1, 0) + to_west * pltpu.roll(mid, 1, 0)
            new = new + to_north * pltpu.roll(mid, ny - 1, 1) + to_south * pltpu.roll(mid, 1, 1)
            if l + 1 < levels:
                new = new + to_upper * v_ref[c, l + 1]
            if l > 0:
                new = new + to_lower * v_ref[c, l - 1]
            vn_ref[c, l] = new
            nxt.append(new)
        parts[l * 9 * nx : (l + 1) * 9 * nx, :] = three_parts(jnp.concatenate(nxt, axis=0))

    lanes = lax.broadcasted_iota(jnp.int32, (1, 2 * LANES), 1)
    position = lax.broadcasted_iota(jnp.int32, (ny, 2 * LANES), 0)
    half = levels // 2
    span = half * 9 * nx
    for arrival in arrivals:
        arrival.wait()

    def chunk(k):
        level_of, x_of, y_of = [lane_values(spots, n, k * CHUNK, lanes) for n in range(3)]
        where_ref[k, 0:1] = level_of
        where_ref[k, 1:2] = x_of
        source = 2 * (y_of + lanes % PY) + lanes // LANES
        picks = jnp.where(position == source, 1.0, 0.0).astype(BF16)
        picks_ref[k] = picks
        for part in range(2):
            got = mm(parts[part * span : (part + 1) * span, :], picks)
            for i in range(half):
                at = i * 9 * nx
                chosen[part * half + i] = fold_parts(got[at : at + 9 * nx], 3 * nx)
        for c in range(3):
            take = slice(c * nx, (c + 1) * nx)
            kept = shift_down([chosen[l, take, :] for l in range(levels)], level_of, PZ)
            for l in range(PZ):
                cells_ref[k, l, c] = x_window(kept[l], x_of)

    each(chunks, chunk)
    ch_rows = 9 * PZ * 8
    r = lax.broadcasted_iota(jnp.int32, (ch_rows, KIN * FIELD_ROWS), 0)
    col = lax.broadcasted_iota(jnp.int32, (ch_rows, KIN * FIELD_ROWS), 1)
    channel = r >> 5
    slot = jnp.where(channel < 3, channel, channel + 5)
    goal = ((((r >> 3) & 3) * PX + ((r & 7) >> 1)) * FIELD_ROWS) + slot
    goal_ref[...] = jnp.where((col == goal) & ((r & 1) == 0), 1.0, 0.0).astype(BF16)


def beyond_terms(near_ref, far_ref, plane_ref, first_ref, second_ref, beyond_ref):
    odd = lax.axis_index("sec") % 2 == 1
    upper_band = lax.axis_index("band") == 1
    share = TIME_STEP * VISCOSITY
    slope = TIME_STEP * 0.5
    u_near, u_far, w_plane = near_ref[0], far_ref[0], plane_ref[2]
    at_west = share + slope * jnp.where(odd, u_near, u_far)
    at_east = share - slope * jnp.where(odd, u_far, u_near)
    at_plane = jnp.where(upper_band, share + slope * w_plane, share - slope * w_plane)
    west, east, plane = [], [], []
    for c in range(3):
        west.append(jnp.where(odd, first_ref[c], second_ref[c]) * at_west)
        east.append(jnp.where(odd, second_ref[c], first_ref[c]) * at_east)
        plane.append(beyond_ref[c] * at_plane)
    return upper_band, west, east, plane


def crop_kernel(
    where_ref, cells_ref, picks_ref, goal_ref, near_ref, far_ref, plane_ref, first_ref, second_ref, beyond_ref, crop_ref
):
    upper_band, west, east, plane = beyond_terms(near_ref, far_ref, plane_ref, first_ref, second_ref, beyond_ref)
    chunks = cells_ref.shape[0]
    levels, nx = west[0].shape[0], plane[0].shape[0]
    last_level, last_x = levels - PZ, nx // 2 - PX
    terms = three_parts(jnp.concatenate(west + east + plane, axis=0))
    lanes = lax.broadcasted_iota(jnp.int32, (1, 2 * LANES), 1)
    row = lax.broadcasted_iota(jnp.int32, (2 * PX, 2 * LANES), 0)

    def chunk(k):
        level_of = where_ref[k, 0:1]
        x_of = where_ref[k, 1:2]
        got = fold_parts(mm(terms, picks_ref[k]), 6 * levels + 3 * nx)
        window = [[None] * 3 for _ in range(PZ)]
        low_plane = upper_band & (level_of == 0)
        high_plane = jnp.logical_not(upper_band) & (level_of == last_level)
        for c in range(3):
            sides = []
            for side in (c, 3 + c):
                kept = got[side * levels : (side + 1) * levels]
                step = 1 << last_level.bit_length()
                while step > 1:
                    step //= 2
                    kept = jnp.where((level_of & step) != 0, pltpu.roll(kept, levels - step, 0), kept)
                sides.append(kept)
            at_west = jnp.where(x_of == 0, sides[0], 0.0)
            at_east = jnp.where(x_of == last_x, sides[1], 0.0)
            at_plane = x_window(got[6 * levels + c * nx : 6 * levels + (c + 1) * nx], x_of)
            for l in range(PZ):
                outer = jnp.where(row == 0, at_west[l : l + 1], 0.0) + jnp.where(
                    row == 2 * PX - 1, at_east[l : l + 1], 0.0
                )
                value = cells_ref[k, l, c] + outer
                if l == 0:
                    value = value + jnp.where(low_plane, at_plane, 0.0)
                if l == PZ - 1:
                    value = value + jnp.where(high_plane, at_plane, 0.0)
                window[l][c] = value

        def box(cells):
            pair = cells[:, :LANES] + cells[:, LANES:]
            return (pair + pltpu.roll(pair, 2 * PX - 1, 0)) * 0.25

        rows = [None] * (9 * PZ)
        for l in range(PZ):
            means = [box(cells) for cells in window[l]]
            for c in range(3):
                rows[c * PZ + l] = means[c]
            for n, (i, j) in enumerate(PAIRS):
                rows[(3 + n) * PZ + l] = box(window[l][i] * window[l][j]) - means[i] * means[j]
        fields = jnp.concatenate(rows, axis=0).astype(BF16)
        crop_ref[k] = tn(fields, goal_ref[...]).astype(BF16)

    each(chunks, chunk)


def finish_kernel(
    vn_ref, near_ref, far_ref, plane_ref, first_ref, second_ref, beyond_ref, out_ref, done, sems
):
    upper_band, west, east, plane = beyond_terms(near_ref, far_ref, plane_ref, first_ref, second_ref, beyond_ref)
    _, levels, nx, ny = vn_ref.shape
    row = lax.broadcasted_iota(jnp.int32, (nx, ny), 0)
    copies = []
    for l in range(levels):
        for c in range(3):
            value = vn_ref[c, l] + jnp.where(
                row == 0, west[c][l : l + 1], jnp.where(row == nx - 1, east[c][l : l + 1], 0.0)
            )
            if l == 0:
                value = value + jnp.where(upper_band, plane[c], 0.0)
            if l == levels - 1:
                value = value + jnp.where(upper_band, 0.0, plane[c])
            done[c, l] = value
        copy = pltpu.make_async_copy(done.at[:, l], out_ref.at[:, l], sems.at[l])
        copy.start()
        copies.append(copy)
    for copy in copies:
        copy.wait()


def cost(flops, moved):
    return pl.CostEstimate(flops=flops, bytes_accessed=moved, transcendentals=0)


def inner_step(level, cx, cy, velocity):
    samples = level.size
    chunks = samples // CHUNK
    _, levels, nx, ny = velocity.shape
    return pl.pallas_call(
        inner_kernel,
        out_shape=(
            jax.ShapeDtypeStruct(velocity.shape, F32),
            jax.ShapeDtypeStruct((chunks, PZ, 3, 2 * PX, 2 * LANES), F32),
            jax.ShapeDtypeStruct((chunks, ny, 2 * LANES), BF16),
            jax.ShapeDtypeStruct((9 * PZ * 8, KIN * FIELD_ROWS), BF16),
            jax.ShapeDtypeStruct((chunks, 8, 2 * LANES), jnp.int32),
        ),
        in_specs=[HBM, HBM, HBM, VMEM],
        out_specs=(VMEM,) * 5,
        scratch_shapes=[
            pltpu.VMEM((levels * 9 * nx, ny), BF16),
            pltpu.VMEM((levels, 3 * nx, 2 * LANES), F32),
            pltpu.SMEM((3, 1, samples), jnp.int32),
            pltpu.SemaphoreType.DMA((3,)),
        ],
        compiler_params=small_params(14 + 2 * chunks),
        cost_estimate=cost(3 * 10**9, 8 * 10**6),
        name="inner_step",
    )(*[in_hbm(x.reshape(1, samples)) for x in (level, cx, cy)], velocity)


def cut_crops(inner, edges):
    _, cells, picks, goal, where = inner
    chunks = cells.shape[0]
    return pl.pallas_call(
        crop_kernel,
        out_shape=jax.ShapeDtypeStruct((chunks, LANES, KIN * FIELD_ROWS), BF16),
        in_specs=[VMEM] * 10,
        out_specs=VMEM,
        compiler_params=small_params(6 + 2 * chunks),
        cost_estimate=cost(10**9, 3 * 10**6),
        name="cut_crops",
    )(where, cells, picks, goal, *edges)


def finish_step(inner, edges):
    vn = inner[0]
    return pl.pallas_call(
        finish_kernel,
        out_shape=jax.ShapeDtypeStruct(vn.shape, F32),
        in_specs=[VMEM] * 7,
        out_specs=HBM,
        scratch_shapes=[pltpu.VMEM(vn.shape, F32), pltpu.SemaphoreType.DMA((vn.shape[1],))],
        compiler_params=small_params(10),
        cost_estimate=cost(2 * 10**9, 4 * 10**6),
        name="finish_step",
    )(vn, *edges)


def train_kernel(
    factor, count_ref, batch_ref, gain_ref, shift_ref, w1_ref, w2f_ref, w2b_ref, w3f_ref, w3b_ref,
    packed_ref, sx, hidden, s2, h2, act2, tap_out, des, dys, dn, flat, g2, small, out_ref,
):
    chunks = batch_ref.shape[0]
    width = KIN * LANES
    band = PX * LANES
    count = count_ref[0]
    points = count.astype(F32) * (KIN * PY)
    lane = lax.broadcasted_iota(jnp.int32, (1, LANES), 1)
    y = lane % PY
    inside = {-1: y > 0, 1: y < PY - 1}

    def live(k):
        return jnp.where(k * CHUNK + lane // PY < count, 1.0, 0.0)

    def shifted(block, dy):
        if dy == 0:
            return block
        return jnp.where(inside[dy], pltpu.roll(block, (-dy) % LANES, 1), 0.0)

    def at(l, x):
        return slice((l * PX + x) * LANES, (l * PX + x + 1) * LANES)

    def stack_taps(blocks, sign, store):
        moved = {dy: [shifted(block, dy) for block in blocks] for dy in OFFSETS}
        zero = jnp.zeros((8, LANES), F32)
        for l in range(PZ):
            for x in range(PX):
                column = []
                for dz, dx, dy in TAPS:
                    lz, xx = l + sign * dz, x + sign * dx
                    ok = 0 <= lz < PZ and 0 <= xx < PX
                    column.append(moved[sign * dy][lz * PX + xx] if ok else zero)
                store(at(l, x), jnp.concatenate(column, axis=0).astype(BF16))

    def stack_rows(block_of, sign):
        for l in range(PZ):
            for x in range(PX):
                block = block_of(l, x)
                for i, dy in enumerate(OFFSETS):
                    s2[i * CH : (i + 1) * CH, at(l, x)] = shifted(block, sign * dy).astype(BF16)

    def plane_products(weights, sign, target):
        for l in range(PZ):
            got = mm(weights[...], s2[:, l * band : (l + 1) * band])
            for i, dz in enumerate(OFFSETS):
                goal = l - sign * dz
                if not 0 <= goal < PZ:
                    continue
                for x in range(PX):
                    piece = None
                    for j, dx in enumerate(OFFSETS):
                        source = x + sign * dx
                        if 0 <= source < PX:
                            n = i * 3 + j
                            term = got[n * CH : (n + 1) * CH, source * LANES : (source + 1) * LANES]
                            piece = term if piece is None else piece + term
                    if l == max(0, goal - 1):
                        target[:, at(goal, x)] = piece
                    else:
                        target[:, at(goal, x)] += piece

    def column(row):
        eye = lax.broadcasted_iota(jnp.int32, (CH, CH), 0) == lax.broadcasted_iota(jnp.int32, (CH, CH), 1)
        return jnp.sum(jnp.where(eye, row, 0.0), axis=1, keepdims=True)

    def line(col):
        eye = lax.broadcasted_iota(jnp.int32, (CH, CH), 0) == lax.broadcasted_iota(jnp.int32, (CH, CH), 1)
        return jnp.sum(jnp.where(eye, col, 0.0), axis=0, keepdims=True)

    gain = column(gain_ref[...])
    shift = column(shift_ref[...])
    eye_rows = KIN * FIELD_ROWS
    eye = jnp.where(
        lax.broadcasted_iota(jnp.int32, (eye_rows, eye_rows), 0)
        == lax.broadcasted_iota(jnp.int32, (eye_rows, eye_rows), 1),
        1.0,
        0.0,
    ).astype(BF16)

    flat[:, 0:LANES] = jnp.zeros((CH, LANES), F32)

    def first_pass(k):
        turned = nt(eye, batch_ref[k])
        blocks = [turned[b * FIELD_ROWS : b * FIELD_ROWS + 8] for b in range(KIN)]

        def store(where, value):
            sx[k, :, where] = value

        stack_taps(blocks, 1, store)
        mask = live(k)
        total = flat[:, 0:LANES]
        for l in range(PZ):
            got = mm(w1_ref[...], sx[k, :, l * band : (l + 1) * band])
            hidden[k, :, l * band : (l + 1) * band] = got
            for x in range(PX):
                total = total + got[:, x * LANES : (x + 1) * LANES] * mask
        flat[:, 0:LANES] = total

    each(chunks, first_pass)
    average = jnp.sum(flat[:, 0:LANES], axis=1, keepdims=True) / points
    flat[:, 0:LANES] = jnp.zeros((CH, LANES), F32)

    def second_pass(k):
        mask = live(k)
        total = flat[:, 0:LANES]
        for b in range(KIN):
            where = slice(b * LANES, (b + 1) * LANES)
            centred = hidden[k, :, where] - average
            hidden[k, :, where] = centred
            total = total + centred * centred * mask
        flat[:, 0:LANES] = total

    each(chunks, second_pass)
    variance = jnp.sum(flat[:, 0:LANES], axis=1, keepdims=True) / points
    inverse = lax.rsqrt(variance + EPSILON)

    g2[...] = jnp.zeros_like(g2)
    small[...] = jnp.zeros_like(small)
    flat[:, 0 : 2 * LANES] = jnp.zeros((CH, 2 * LANES), F32)
    flat[0:8, 2 * LANES : 3 * LANES] = jnp.zeros((8, LANES), F32)

    def main_pass(k):
        mask = live(k)

        def act_first(l, x):
            normed = hidden[k, :, at(l, x)] * inverse * gain + shift
            return normed * jax.nn.sigmoid(normed)

        stack_rows(act_first, 1)
        plane_products(w2f_ref, 1, h2)
        for b in range(KIN):
            where = slice(b * LANES, (b + 1) * LANES)
            pre = h2[:, where]
            act2[:, where] = (pre * jax.nn.sigmoid(pre)).astype(BF16)
        for l in range(PZ):
            where = slice(l * band, (l + 1) * band)
            tap_out[:, where] = mm(w3f_ref[...], act2[:, where])
        turned = nt(eye, batch_ref[k])
        errors = []
        lost = flat[0:8, 2 * LANES : 3 * LANES]
        for l in range(PZ):
            for x in range(PX):
                sums = {}
                for t, (dz, dx, dy) in enumerate(TAPS):
                    lz, xx = l + dz, x + dx
                    if 0 <= lz < PZ and 0 <= xx < PX:
                        piece = tap_out[t * 8 : (t + 1) * 8, at(lz, xx)]
                        sums[dy] = sums[dy] + piece if dy in sums else piece
                output = sums[0] + shifted(sums[-1], -1) + shifted(sums[1], 1)
                b = l * PX + x
                error = (output - turned[b * FIELD_ROWS + 8 : b * FIELD_ROWS + 16]) * mask
                lost = lost + error * error
                errors.append(2.0 * factor * error)
        flat[0:8, 2 * LANES : 3 * LANES] = lost

        def store(where, value):
            des[:, where] = value

        stack_taps(errors, -1, store)
        small[:, 0:CH] += nt(des[...], act2[...])
        for l in range(PZ):
            got = mm(w3b_ref[...], des[:, l * band : (l + 1) * band])
            for x in range(PX):
                where = at(l, x)
                cot = got[:, x * LANES : (x + 1) * LANES].astype(BF16).astype(F32)
                pre = h2[:, where]
                sig = jax.nn.sigmoid(pre)
                h2[:, where] = cot * (sig * (1.0 + pre * (1.0 - sig)))
        zero = jnp.zeros((CH, LANES), BF16)
        for l in range(PZ):
            for x in range(PX):
                piece = h2[:, at(l, x)].astype(BF16)
                for n in range(9):
                    goal, gx = l + n // 3 - 1, x + n % 3 - 1
                    if 0 <= goal < PZ and 0 <= gx < PX:
                        dys[n * CH : (n + 1) * CH, at(goal, gx)] = piece
                    source, sx_at = l - n // 3 + 1, x - n % 3 + 1
                    if not (0 <= source < PZ and 0 <= sx_at < PX):
                        dys[n * CH : (n + 1) * CH, at(l, x)] = zero
        g2[...] += nt(dys[...], s2[...])
        stack_rows(lambda l, x: h2[:, at(l, x)], -1)
        plane_products(w2b_ref, -1, act_cot)
        by_gain = flat[:, 0:LANES]
        by_shift = flat[:, LANES : 2 * LANES]
        for b in range(KIN):
            where = slice(b * LANES, (b + 1) * LANES)
            cot = act_cot[:, where].astype(BF16).astype(F32)
            normal = hidden[k, :, where] * inverse
            normed = normal * gain + shift
            sig = jax.nn.sigmoid(normed)
            d_normed = cot * (sig * (1.0 + normed * (1.0 - sig)))
            by_gain = by_gain + d_normed * normal
            by_shift = by_shift + d_normed
            dn[k, :, where] = d_normed
        flat[:, 0:LANES] = by_gain
        flat[:, LANES : 2 * LANES] = by_shift

    act_cot = tap_out.at[0:CH]
    each(chunks, main_pass)
    grad_gain = jnp.sum(flat[:, 0:LANES], axis=1, keepdims=True)
    grad_shift = jnp.sum(flat[:, LANES : 2 * LANES], axis=1, keepdims=True)
    loss = jnp.sum(flat[0:8, 2 * LANES : 3 * LANES]) * factor

    from_mean = -inverse * (gain * grad_shift) / points
    from_variance = -(gain * grad_gain) * inverse * inverse / points
    scale = gain * inverse

    out_ref[...] = jnp.zeros_like(out_ref)

    def last_pass(k):
        mask = live(k)
        for b in range(KIN):
            where = slice(b * LANES, (b + 1) * LANES)
            d_hidden = dn[k, :, where] * scale + mask * (from_mean + from_variance * hidden[k, :, where])
            act2[:, where] = d_hidden.astype(BF16)
        small[:, CH:LANES] += nt(sx[k], act2[...])

    each(chunks, last_pass)

    half = MID_ROWS // 2
    out_ref[0:MID_ROWS, :] = g2[:, 0:LANES]
    out_ref[HALF_BASE : HALF_BASE + half, 0:CH] = g2[0:half, LANES:]
    out_ref[HALF_BASE : HALF_BASE + half, CH:LANES] = g2[half:, LANES:]
    both = [small[pl.ds(o, 27, stride=8), :] for o in range(6)]
    planes = [pair[:, 0:CH] for pair in both] + [pair[:, CH:LANES] for pair in both[0:3]]
    for n, plane in enumerate(planes):
        base = PLANE_BASE + (n // 2) * PLANE_STEP
        side = (n % 2) * CH
        out_ref[base : base + 27, side : side + CH] = plane
    out_ref[MISC_BASE : MISC_BASE + 1, 0:CH] = line(grad_gain)
    out_ref[MISC_BASE : MISC_BASE + 1, CH:LANES] = line(grad_shift)
    out_ref[MISC_BASE + 1 : MISC_BASE + 2, :] = jnp.full((1, LANES), loss, F32)
    devices = packed_ref.shape[0]
    mid, rest, top, _ = shares(devices)
    for d in range(devices):
        own = out_ref[PLANE_BASE + d * rest : PLANE_BASE + (d + 1) * rest, :]
        high, low = two_parts(own)
        both = jnp.concatenate([out_ref[d * mid : (d + 1) * mid, :], own], axis=0)
        packed_ref[d, 0:top, :] = fill(both, top).astype(BF16)
        packed_ref[d, top:, :] = fill(low.astype(F32), packed_ref.shape[1] - top).astype(BF16)


def combine_kernel(parts_ref, out_ref):
    devices = parts_ref.shape[0]
    mid, rest, top, rows = shares(devices)
    total = parts_ref[0].astype(F32)
    for d in range(1, devices):
        total = total + parts_ref[d].astype(F32)
    own = total[mid : mid + rest] + total[top : top + rest]
    high, low = two_parts(own)
    whole = jnp.concatenate(
        [fill(jnp.concatenate([total[0:mid], own], axis=0), top), fill(low.astype(F32), rows - top)], axis=0
    ).astype(BF16)
    for d in range(devices):
        out_ref[d] = whole


def combine(parts):
    return pl.pallas_call(
        combine_kernel,
        out_shape=jax.ShapeDtypeStruct(parts.shape, BF16),
        in_specs=[VMEM],
        out_specs=VMEM,
        compiler_params=small_params(8),
        name="combine",
    )(parts)


def train(factor, devices, count, batch, gain, shift, weights):
    chunks = batch.shape[0]
    width = KIN * LANES
    return pl.pallas_call(
        functools.partial(train_kernel, factor),
        out_shape=jax.ShapeDtypeStruct((devices, shares(devices)[3], LANES), BF16),
        in_specs=[SMEM] + [VMEM] * 8,
        out_specs=VMEM,
        scratch_shapes=[
            pltpu.VMEM((chunks, TAP_ROWS, width), BF16),
            pltpu.VMEM((chunks, CH, width), F32),
            pltpu.VMEM((3 * CH, width), BF16),
            pltpu.VMEM((CH, width), F32),
            pltpu.VMEM((CH, width), BF16),
            pltpu.VMEM((TAP_ROWS, width), F32),
            pltpu.VMEM((TAP_ROWS, width), BF16),
            pltpu.VMEM((9 * CH, width), BF16),
            pltpu.VMEM((chunks, CH, width), F32),
            pltpu.VMEM((CH, 3 * LANES), F32),
            pltpu.VMEM((9 * CH, 3 * CH), F32),
            pltpu.VMEM((TAP_ROWS, LANES), F32),
            pltpu.VMEM((padded_rows(devices)[1], LANES), F32),
        ],
        compiler_params=small_params(20 + 4 * chunks),
        name="train_step",
    )(count, batch, gain, shift, *weights)


def update_kernel(
    whole_ref, wf_ref, gain_ref, shift_ref, wm_ref, wl_ref, nf_ref, ng_ref, ns_ref, nm_ref, nl_ref, loss_ref, grad_ref
):
    devices = whole_ref.shape[0]
    mid, rest, top, _ = shares(devices)
    for d in range(devices):
        grad_ref[d * mid : (d + 1) * mid, :] = whole_ref[d, 0:top, :].astype(F32)[0:mid]
    for d in range(devices):
        high = whole_ref[d, 0:top, :].astype(F32)[mid : mid + rest]
        low = whole_ref[d, top:, :].astype(F32)[0:rest]
        grad_ref[PLANE_BASE + d * rest : PLANE_BASE + (d + 1) * rest, :] = high + low
    half = MID_ROWS // 2
    fold = grad_ref[HALF_BASE : HALF_BASE + half, :]
    last = jnp.concatenate([fold[:, :CH], fold[:, CH:]], axis=0)
    for zx in range(9):
        rows_at = slice(zx * CH, (zx + 1) * CH)
        block = grad_ref[rows_at, :]
        nm_ref[zx * 3] = wm_ref[zx * 3] - LEARNING * block[:, :CH]
        nm_ref[zx * 3 + 1] = wm_ref[zx * 3 + 1] - LEARNING * block[:, CH:]
        nm_ref[zx * 3 + 2] = wm_ref[zx * 3 + 2] - LEARNING * last[rows_at]
    for n in range(9):
        base = PLANE_BASE + (n // 2) * PLANE_STEP
        side = (n % 2) * CH
        plane = grad_ref[base : base + 27, side : side + CH]
        if n < 6:
            nl_ref[n] = wl_ref[n] - LEARNING * plane
        else:
            nf_ref[n - 6] = wf_ref[n - 6] - LEARNING * plane
    misc = grad_ref[MISC_BASE : MISC_BASE + 1, :]
    ng_ref[...] = gain_ref[...] - LEARNING * misc[:, :CH]
    ns_ref[...] = shift_ref[...] - LEARNING * misc[:, CH:]
    loss_ref[...] = grad_ref[MISC_BASE + 1 : MISC_BASE + 2, 0:1]


def update(whole, wf, gain, shift, wm, wl):
    shapes = [wf, gain, shift, wm, wl]
    return pl.pallas_call(
        update_kernel,
        out_shape=tuple(jax.ShapeDtypeStruct(w.shape, F32) for w in shapes) + (jax.ShapeDtypeStruct((1, 1), F32),),
        in_specs=[VMEM] * 6,
        out_specs=(VMEM,) * 6,
        scratch_shapes=[pltpu.VMEM((padded_rows(whole.shape[0])[1], LANES), F32)],
        compiler_params=small_params(12),
        name="update",
    )(whole, *shapes)


def exchange(rows):
    return lax.all_to_all(rows, ("sec", "band"), split_axis=0, concat_axis=0, tiled=True)


def on_device(
    velocity, crop_level, crop_x, crop_y, live_count, w_first, norm_gain, norm_shift, w_middle, w_last
):
    sources = lax.axis_size("sec")
    bands = lax.axis_size("band")
    assert bands == 2 and sources % 2 == 0
    groups = sources * bands
    wf = jnp.transpose(w_first, (2, 0, 1))
    wl = jnp.transpose(w_last, (1, 0, 2))
    weights = arrange_weights(wf, w_middle, wl)

    held, near, far, plane = edges_step(velocity)
    first = lax.ppermute(near, "sec", [(i, i ^ 1) for i in range(sources)])
    second = lax.ppermute(far, "sec", [(i, ((i + 1) ^ 1) - 1) for i in range(1, sources - 1)])
    beyond = lax.ppermute(plane, "band", [(0, 1), (1, 0)])

    inner = inner_step(crop_level, crop_x, crop_y, held)
    edges = (near, far, plane, first, second, beyond)
    crops = cut_crops(inner, edges)
    velocity_next = finish_step(inner, edges)
    crops = crops.reshape(sources, PY, KIN * FIELD_ROWS)
    batch = lax.all_to_all(crops, "sec", split_axis=0, concat_axis=0, tiled=True)
    batch, velocity_next = lax.optimization_barrier((batch, velocity_next))
    batch = batch.reshape(sources // CHUNK, LANES, KIN * FIELD_ROWS)
    factor = 1.0 / (6.0 * PZ * PX * PY * (groups * sources * 5 // 8))
    gain, shift = norm_gain.reshape(1, CH), norm_shift.reshape(1, CH)
    parts = train(factor, groups, live_count, batch, gain, shift, weights)
    whole = exchange(combine(exchange(parts)))
    nf, ng, ns, nm, nl, loss = update(whole, wf, gain, shift, w_middle, wl)
    return (
        velocity_next,
        jnp.transpose(nf, (1, 2, 0)),
        ng.reshape(CH),
        ns.reshape(CH),
        nm,
        jnp.transpose(nl, (1, 0, 2)),
        loss.reshape(()),
    )


def solution(mesh):
    in_specs = (
        P(None, "band", "sec", None),
        P("sec", "band", None),
        P("sec", "band", None),
        P("sec", "band", None),
        P(("sec", "band")),
        P(),
        P(),
        P(),
        P(),
        P(),
    )
    out_specs = (P(None, "band", "sec", None), P(), P(), P(), P(), P(), P())
    return jax.shard_map(
        on_device, mesh=mesh, in_specs=in_specs, out_specs=out_specs, check_vma=False
    )
```

time: 80.8 us -> 62.3 us (0.77)
  blocking collectives: 36.6 us -> 27.8 us
  Pallas kernels: 17.2 us -> 13.8 us
  local copies, waits for them, and re-layouts: 4.06 us -> 1.44 us
  other arithmetic: 1.62 us -> 0 us
  starting transfers between devices: 14.1 us -> 12.7 us
    all_to_all x2, blocking collectives: 36.6 us -> 27.8 us  [exchange(): lax.all_to_all(rows, ('sec', 'band'), split_axis=0, concat_axis=0, tiled=...]
    slice x2 -> x0, local copies, waits for them, and re-layouts: 2.74 us -> none  [the longest x1 1.55 us: on_device(): head, tail = (velocity[:, :, 0, :], velocity[:, :, -1, :])]
    pallas_call x1, Pallas kernels: 7.5 us -> 5.48 us  [train(): pl.pallas_call(functools.partial(train_kernel, factor), out_shape=jax.Sha...]
    pallas_call x1 -> x5, Pallas kernels: 4.96 us -> 6.92 us  [the longest x1 2.58 us: inner_step(): pl.pallas_call(inner_kernel, out_shape=(jax.ShapeDtypeStruct(velocity.sha...]
    pallas_call x1, Pallas kernels: 2.17 us -> 0.29 us  [arrange_weights(): pl.pallas_call(weights_kernel, out_shape=(jax.ShapeDtypeStruct((CH, TAP_R...]
    all_to_all x1, starting transfers between devices: 10.4 us -> 8.95 us  [on_device(): lax.all_to_all(crops, 'sec', split_axis=0, concat_axis=0, tiled=True)]
    pallas_call x1, Pallas kernels: 2.52 us -> 1.12 us  [update(): pl.pallas_call(update_kernel, out_shape=tuple((jax.ShapeDtypeStruct(w.sha...]
    select_n x2 -> x0, other arithmetic: 0.98 us -> none  [the longest x1 0.96 us: on_device(): plane = jnp.where(band == 0, velocity[:, -1], velocity[:, 0])]
  transfers between devices with their start and end apart: 4 -> 4, of which waited for: 3 -> 1; matrix products, arithmetic and copies ran while one was open for 2% -> 0% of each run, Pallas kernels for 3% -> 7%
where the time goes in v1:
time: 62.3 us; the launch traced here: 62 us
  blocking collectives  27.8 us (45%)
  Pallas kernels  13.8 us (22%)
  starting transfers between devices  12.7 us (20%)
  waiting for transfers between devices  4.76 us (8%)
  local copies, waits for them, and re-layouts  1.44 us (2%)
  between operations  1.43 us (2%)
    all_to_all x2, blocking collectives, exchange(): lax.all_to_all(rows, ('sec', 'band'), split_axis=0, concat_axis=0, tiled=...  27.8 us
    all_to_all x1, starting transfers between devices, on_device(): lax.all_to_all(crops, 'sec', split_axis=0, concat_axis=0, tiled=True)  8.95 us
    pallas_call x1, Pallas kernels, train(): pl.pallas_call(functools.partial(train_kernel, factor), out_shape=jax.Sha...  5.48 us
    all_to_all x1, waiting for transfers between devices, on_device(): lax.all_to_all(crops, 'sec', split_axis=0, concat_axis=0, tiled=True)  4.75 us
    ppermute x1, starting transfers between devices, on_device(): first = lax.ppermute(near, 'sec', [(i, i ^ 1) for i in range(sources)])  3.03 us
    pallas_call x1, Pallas kernels, inner_step(): pl.pallas_call(inner_kernel, out_shape=(jax.ShapeDtypeStruct(velocity.sha...  2.58 us
    pallas_call x1, Pallas kernels, edges_step(): pl.pallas_call(edges_kernel, out_shape=(jax.ShapeDtypeStruct(velocity.sha...  1.66 us
    unnamed x14, local copies, waits for them, and re-layouts  1.44 us
  transfers between devices with their start and end apart: 4, of which 1 were waited for; matrix products, arithmetic and copies ran while one was open for 0% of the time, Pallas kernels for 7%

profile of v1, /device:TPU:0, one launch (start us, length us, event | category | flops | bytes accessed | tf_op | source)
XLA Modules:
  0.0 62.0 jit_solution(16528263628699744523)
XLA Ops:
  0.6 1.7 %edges_step.1 = (f32[3,16,16,512]{3,2,1,0:T(8,128)S(1)}, f32[3,16,512]{2,1,0:T(8,128)S(1)}, f32[3,16,512]{2,1,0:T(8,128)S(1)}, f32[3,16,512]{2,1,0:T(8,128)S(1)}) custom-call(f32[3,16,16,512]{3,2,1,0:T(8,128)} %source_ref.1), custom_call_target="tpu_custom_call" | custom-call | flops 1000000 | bytes 3000000 | tf_op jit(solution)/shard_map/edges_step/pallas_call | solution.py:187
  2.3 3.0 %collective-permute-start = (f32[3,16,512]{2,1,0:T(8,128)S(1)}, f32[3,16,512]{2,1,0:T(8,128)S(1)}, u32[]{:S(2)}, u32[]{:S(2)}) collective-permute-start(f32[3,16,512]{2,1,0:T(8,128)S(1)} %get-tuple-element.34.near_ref), channel_id=1, source_target_pairs={{0,2},{2,0},{4,6},{6,4},{8,10},{10,8},{12,14},{14,12},{16,18},{18,... | collective-permute-start | bytes 294920 | tf_op jit(solution)/shard_map/ppermute | solution.py:788
  5.3 0.7 %collective-permute-start.1 = (f32[3,16,512]{2,1,0:T(8,128)S(1)}, f32[3,16,512]{2,1,0:T(8,128)S(1)}, u32[]{:S(2)}, u32[]{:S(2)}) collective-permute-start(f32[3,16,512]{2,1,0:T(8,128)S(1)} %get-tuple-element.35.far_ref), channel_id=1, source_target_pairs={{2,4},{4,2},{6,8},{8,6},{10,12},{12,10},{14,16},{16,14},{18,20},{2... | collective-permute-start | bytes 294920 | tf_op jit(solution)/shard_map/ppermute | solution.py:789
  6.0 0.1 collective-permute-start.2
  6.1 0.0 copy-start
  6.1 0.0 copy-start.1
  6.1 0.0 copy-start.2
  6.1 2.6 %inner_step.1 = (f32[3,16,16,512]{3,2,1,0:T(8,128)S(1)}, f32[1,4,3,8,256]{4,3,2,1,0:T(8,128)S(1)}, bf16[1,512,256]{2,1,0:T(8,128)(2,1)S(1)}, bf16[288,256]{1,0:T(8,128)(2,1)S(1)}, s32[1,8,256]{2,1,0:T(8,128)S(1)}) custom-call(s32[1,16]{1,0:T(1,128)} %bitcast.25, s32[1,16]{1,0:T(1,128)} %bitcast.26, s32[1,16]{1,0:T(1,128)} %bitcast.27, ...), custom_call_target="tpu_custom_call" | custom-call | flops 3000000000 | bytes 8000000 | tf_op jit(solution)/shard_map/inner_step/pallas_call | solution.py:376
  8.7 0.0 copy-start.5
  9.4 0.0 copy-done
  9.4 0.0 copy-done.1
  9.4 0.0 copy-done.2
  9.4 0.3 arrange_weights.1
  9.7 0.0 collective-permute-done.first_ref
  9.7 0.0 collective-permute-done.1.second_ref
  9.7 0.0 collective-permute-done.2.beyond_ref
  9.7 1.3 %cut_crops.1 = bf16[1,128,256]{2,1,0:T(8,128)(2,1)} custom-call(s32[1,8,256]{2,1,0:T(8,128)S(1)} %get-tuple-element.30.where_ref, f32[1,4,3,8,256]{4,3,2,1,0:T(8,128)S(1)} %get-tuple-element.31.cells_ref, bf16[1,512,256]{2,1,0:T(8,128)(2,1)S(1)} %get-tuple-element.32.picks_ref, bf16[288,256]{1,0:T(8,128)(2,1)S(1)} %get-tuple-element.33.goal_ref, ...), custom_call_target="tpu_custom_call" | custom-call | flops 1000000000 | bytes 3000000 | tf_op jit(solution)/shard_map/cut_crops/pallas_call | solution.py:402
  11.0 0.0 copy-done.5
  11.0 9.0 %all-to-all-start = ((bf16[16,8,256]{2,1,0:T(8,128)(2,1)}), bf16[16,8,256]{2,1,0:T(8,128)(2,1)S(1)}, u32[]{:S(2)}, u32[]{:S(2)}) async-start(bf16[16,8,256]{2,1,0:T(8,128)(2,1)} %bitcast.3), calls=%async_computation | async-start | bytes 131072 | tf_op jit(solution)/shard_map/all_to_all | solution.py:797
  19.9 0.0 copy-start.6
  20.0 1.4 %copy-done.6 = f32[3,16,16,512]{3,2,1,0:T(8,128)S(1)} copy-done((f32[3,16,16,512]{3,2,1,0:T(8,128)S(1)}, f32[3,16,16,512]{3,2,1,0:T(8,128)}, u32[]{:S(2)}) %copy-start.6) | copy-done | bytes 1572888
  21.4 0.0 copy-start.3
  21.4 0.0 copy-start.4
  21.4 1.4 %finish_step.1 = f32[3,16,16,512]{3,2,1,0:T(8,128)} custom-call(f32[3,16,16,512]{3,2,1,0:T(8,128)S(1)} %copy-done.6, f32[3,16,512]{2,1,0:T(8,128)S(1)} %get-tuple-element.34.near_ref, f32[3,16,512]{2,1,0:T(8,128)S(1)} %get-tuple-element.35.far_ref, f32[3,16,512]{2,1,0:T(8,128)S(1)} %get-tuple-element.36.plane_ref, ...), custom_call_target="tpu_custom_call" | custom-call | flops 2000000000 | bytes 4000000 | tf_op jit(solution)/shard_map/finish_step/pallas_call | solution.py:415
  22.7 4.8 %all-to-all-done = bf16[16,8,256]{2,1,0:T(8,128)(2,1)S(1)} async-done(((bf16[16,8,256]{2,1,0:T(8,128)(2,1)}), bf16[16,8,256]{2,1,0:T(8,128)(2,1)S(1)}, u32[]{:S(2)}, u32[]{:S(2)}) %all-to-all-start) | async-done | bytes 65568 | tf_op jit(solution)/shard_map/all_to_all | solution.py:797
  27.5 0.0 copy-done.3
  27.5 0.0 copy-done.4
  27.5 5.5 %train_step.1 = bf16[32,40,128]{2,1,0:T(8,128)(2,1)S(1)} custom-call(s32[1]{0:T(128)S(6)} %copy.17.count_ref, bf16[1,128,256]{2,1,0:T(8,128)(2,1)S(1)} %bitcast.16, f32[1,64]{1,0:T(1,128)S(1)} %bitcast.19, f32[1,64]{1,0:T(1,128)S(1)} %bitcast.21, bf16[64,216]{1,0:T(8,128)(2,1)S(1)} %get-tuple-element.40.w1_ref, ...), custom_call_target="tpu_custom_call" | custom-call | tf_op jit(solution)/shard_map/train_step/pallas_call | solution.py:700
  33.0 13.8 %all_to_all.15.parts_ref = bf16[32,40,128]{2,1,0:T(8,128)(2,1)S(1)} all-to-all(bf16[32,40,128]{2,1,0:T(8,128)(2,1)S(1)} %train_step.1), channel_id=1, replica_groups=mesh['sec'=16,'band'=2] {'sec','band'}, dimensions={0} | all-to-all | bytes 655360 | tf_op jit(solution)/shard_map/all_to_all | solution.py:773
  46.7 0.1 combine.1
  46.8 14.1 %all_to_all.16.whole_ref = bf16[32,40,128]{2,1,0:T(8,128)(2,1)S(1)} all-to-all(bf16[32,40,128]{2,1,0:T(8,128)(2,1)S(1)} %combine.1), channel_id=1, replica_groups=mesh['sec'=16,'band'=2] {'sec','band'}, dimensions={0} | all-to-all | bytes 655360 | tf_op jit(solution)/shard_map/all_to_all | solution.py:773
  60.9 1.1 %update.1 = (f32[3,27,64]{2,1,0:T(8,128)}, f32[1,64]{1,0:T(1,128)}, f32[1,64]{1,0:T(1,128)}, f32[27,64,64]{2,1,0:T(8,128)}, f32[6,27,64]{2,1,0:T(8,128)}, /*index=5*/f32[1,1]{1,0:T(1,128)}) custom-call(bf16[32,40,128]{2,1,0:T(8,128)(2,1)S(1)} %all_to_all.16.whole_ref, f32[3,27,64]{2,1,0:T(8,128)S(1)} %bitcast.18, f32[1,64]{1,0:T(1,128)S(1)} %bitcast.20, ...), custom_call_target="tpu_custom_call" | custom-call | tf_op jit(solution)/shard_map/update/pallas_call | solution.py:761
Async XLA Ops:
  2.3 7.4 %collective-permute-start = (f32[3,16,512]{2,1,0:T(8,128)S(1)}, f32[3,16,512]{2,1,0:T(8,128)S(1)}, u32[]{:S(2)}, u32[]{:S(2)}) collective-permute-start(f32[3,16,512]{2,1,0:T(8,128)S(1)} %get-tuple-element.34.near_ref), channel_id=1, source_target_pairs={{0,2},{2,0},{4,6},{6,4},{8,10},{10,8},{12,14},{14,12},{16,18},{18,... | collective-permute-start | bytes 294920 | tf_op jit(solution)/shard_map/ppermute | solution.py:788
  5.3 4.4 %collective-permute-start.1 = (f32[3,16,512]{2,1,0:T(8,128)S(1)}, f32[3,16,512]{2,1,0:T(8,128)S(1)}, u32[]{:S(2)}, u32[]{:S(2)}) collective-permute-start(f32[3,16,512]{2,1,0:T(8,128)S(1)} %get-tuple-element.35.far_ref), channel_id=1, source_target_pairs={{2,4},{4,2},{6,8},{8,6},{10,12},{12,10},{14,16},{16,14},{18,20},{2... | collective-permute-start | bytes 294920 | tf_op jit(solution)/shard_map/ppermute | solution.py:789
  6.0 3.7 %collective-permute-start.2 = (f32[3,16,512]{2,1,0:T(8,128)S(1)}, f32[3,16,512]{2,1,0:T(8,128)S(1)}, u32[]{:S(2)}, u32[]{:S(2)}) collective-permute-start(f32[3,16,512]{2,1,0:T(8,128)S(1)} %get-tuple-element.36.plane_ref), channel_id=1, source_target_pairs={{0,1},{1,0},{2,3},{3,2},{4,5},{5,4},{6,7},{7,6},{8,9},{9,8},{10,11... | collective-permute-start | bytes 294920 | tf_op jit(solution)/shard_map/ppermute | solution.py:790
  6.1 3.3 %copy-start = (f32[27,64,64]{2,1,0:T(8,128)S(1)}, f32[27,64,64]{2,1,0:T(8,128)}, u32[]{:S(2)}) copy-start(f32[27,64,64]{2,1,0:T(8,128)} %wm_ref.3) | copy-start | bytes 1327108
  6.1 3.3 %copy-start.1 = (f32[27,6,64]{2,0,1:T(8,128)S(1)}, f32[27,6,64]{2,0,1:T(8,128)}, u32[]{:S(2)}) copy-start(f32[27,6,64]{2,0,1:T(8,128)} %param.19) | copy-start | bytes 124420
  6.1 3.3 %copy-start.2 = (f32[27,64,3]{1,0,2:T(8,128)S(1)}, f32[27,64,3]{1,0,2:T(8,128)}, u32[]{:S(2)}) copy-start(f32[27,64,3]{1,0,2:T(8,128)} %param.15) | copy-start | bytes 62212
  8.7 2.3 %copy-start.5 = (f32[3,16,16,512]{3,2,1,0:T(8,128)}, f32[3,16,16,512]{3,2,1,0:T(8,128)S(1)}, u32[]{:S(2)}) copy-start(f32[3,16,16,512]{3,2,1,0:T(8,128)S(1)} %get-tuple-element.37.vn_ref) | copy-start | bytes 4718596
  11.0 16.5 %all-to-all-start = ((bf16[16,8,256]{2,1,0:T(8,128)(2,1)}), bf16[16,8,256]{2,1,0:T(8,128)(2,1)S(1)}, u32[]{:S(2)}, u32[]{:S(2)}) async-start(bf16[16,8,256]{2,1,0:T(8,128)(2,1)} %bitcast.3), calls=%async_computation | async-start | bytes 131072 | tf_op jit(solution)/shard_map/all_to_all | solution.py:797
  19.9 1.4 %copy-start.6 = (f32[3,16,16,512]{3,2,1,0:T(8,128)S(1)}, f32[3,16,16,512]{3,2,1,0:T(8,128)}, u32[]{:S(2)}) copy-start(f32[3,16,16,512]{3,2,1,0:T(8,128)} %copy-done.5) | copy-start | bytes 4718596
  21.4 6.1 %copy-start.3 = (f32[64]{0:T(128)S(1)}, f32[64]{0:T(128)}, u32[]{:S(2)}) copy-start(f32[64]{0:T(128)} %param.16) | copy-start | bytes 772
  21.4 6.1 %copy-start.4 = (f32[64]{0:T(128)S(1)}, f32[64]{0:T(128)}, u32[]{:S(2)}) copy-start(f32[64]{0:T(128)} %param.17) | copy-start | bytes 772

commit v2 on v1

--- a/solution.py
+++ b/solution.py
@@ -426,7 +426,7 @@
 
 def train_kernel(
     factor, count_ref, batch_ref, gain_ref, shift_ref, w1_ref, w2f_ref, w2b_ref, w3f_ref, w3b_ref,
-    packed_ref, sx, hidden, s2, h2, act2, tap_out, des, dys, dn, flat, g2, small, out_ref,
+    mine_ref, theirs_ref, sx, hidden, s2, s3, h2, act2, tap_out, des, dys, dn, flat, g2, small, out_ref,
 ):
     chunks = batch_ref.shape[0]
     width = KIN * LANES
@@ -460,16 +460,16 @@
                     column.append(moved[sign * dy][lz * PX + xx] if ok else zero)
                 store(at(l, x), jnp.concatenate(column, axis=0).astype(BF16))
 
-    def stack_rows(block_of, sign):
+    def stack_rows(block_of, sign, stack):
         for l in range(PZ):
             for x in range(PX):
                 block = block_of(l, x)
                 for i, dy in enumerate(OFFSETS):
-                    s2[i * CH : (i + 1) * CH, at(l, x)] = shifted(block, sign * dy).astype(BF16)
-
-    def plane_products(weights, sign, target):
+                    stack[i * CH : (i + 1) * CH, at(l, x)] = shifted(block, sign * dy).astype(BF16)
+
+    def plane_products(weights, stack, sign, target):
         for l in range(PZ):
-            got = mm(weights[...], s2[:, l * band : (l + 1) * band])
+            got = mm(weights[...], stack[:, l * band : (l + 1) * band])
             for i, dz in enumerate(OFFSETS):
                 goal = l - sign * dz
                 if not 0 <= goal < PZ:
@@ -487,6 +487,12 @@
                     else:
                         target[:, at(goal, x)] += piece
 
+    def add_to(ref, columns, value):
+        if chunks > 1:
+            ref[:, columns] += value
+        else:
+            ref[:, columns] = value
+
     def column(row):
         eye = lax.broadcasted_iota(jnp.int32, (CH, CH), 0) == lax.broadcasted_iota(jnp.int32, (CH, CH), 1)
         return jnp.sum(jnp.where(eye, row, 0.0), axis=1, keepdims=True)
@@ -542,8 +548,9 @@
     variance = jnp.sum(flat[:, 0:LANES], axis=1, keepdims=True) / points
     inverse = lax.rsqrt(variance + EPSILON)
 
-    g2[...] = jnp.zeros_like(g2)
-    small[...] = jnp.zeros_like(small)
+    if chunks > 1:
+        g2[...] = jnp.zeros_like(g2)
+        small[...] = jnp.zeros_like(small)
     flat[:, 0 : 2 * LANES] = jnp.zeros((CH, 2 * LANES), F32)
     flat[0:8, 2 * LANES : 3 * LANES] = jnp.zeros((8, LANES), F32)
 
@@ -554,8 +561,8 @@
             normed = hidden[k, :, at(l, x)] * inverse * gain + shift
             return normed * jax.nn.sigmoid(normed)
 
-        stack_rows(act_first, 1)
-        plane_products(w2f_ref, 1, h2)
+        stack_rows(act_first, 1, s2)
+        plane_products(w2f_ref, s2, 1, h2)
         for b in range(KIN):
             where = slice(b * LANES, (b + 1) * LANES)
             pre = h2[:, where]
@@ -585,7 +592,7 @@
             des[:, where] = value
 
         stack_taps(errors, -1, store)
-        small[:, 0:CH] += nt(des[...], act2[...])
+        add_to(small, slice(0, CH), nt(des[...], act2[...]))
         for l in range(PZ):
             got = mm(w3b_ref[...], des[:, l * band : (l + 1) * band])
             for x in range(PX):
@@ -594,6 +601,7 @@
                 pre = h2[:, where]
                 sig = jax.nn.sigmoid(pre)
                 h2[:, where] = cot * (sig * (1.0 + pre * (1.0 - sig)))
+        stack_rows(lambda l, x: h2[:, at(l, x)], -1, s3)
         zero = jnp.zeros((CH, LANES), BF16)
         for l in range(PZ):
             for x in range(PX):
@@ -605,9 +613,8 @@
                     source, sx_at = l - n // 3 + 1, x - n % 3 + 1
                     if not (0 <= source < PZ and 0 <= sx_at < PX):
                         dys[n * CH : (n + 1) * CH, at(l, x)] = zero
-        g2[...] += nt(dys[...], s2[...])
-        stack_rows(lambda l, x: h2[:, at(l, x)], -1)
-        plane_products(w2b_ref, -1, act_cot)
+        plane_products(w2b_ref, s3, -1, act_cot)
+        add_to(g2, slice(None), nt(dys[...], s2[...]))
         by_gain = flat[:, 0:LANES]
         by_shift = flat[:, LANES : 2 * LANES]
         for b in range(KIN):
@@ -633,7 +640,12 @@
     from_variance = -(gain * grad_gain) * inverse * inverse / points
     scale = gain * inverse
 
-    out_ref[...] = jnp.zeros_like(out_ref)
+    fixed = out_ref.shape[0] - PLANE_BASE
+    out_ref[PLANE_BASE:, :] = jnp.zeros((fixed, LANES), F32)
+    half = MID_ROWS // 2
+    out_ref[0:MID_ROWS, :] = g2[:, 0:LANES]
+    out_ref[HALF_BASE : HALF_BASE + half, 0:CH] = g2[0:half, LANES:]
+    out_ref[HALF_BASE : HALF_BASE + half, CH:LANES] = g2[half:, LANES:]
 
     def last_pass(k):
         mask = live(k)
@@ -641,14 +653,10 @@
             where = slice(b * LANES, (b + 1) * LANES)
             d_hidden = dn[k, :, where] * scale + mask * (from_mean + from_variance * hidden[k, :, where])
             act2[:, where] = d_hidden.astype(BF16)
-        small[:, CH:LANES] += nt(sx[k], act2[...])
+        add_to(small, slice(CH, LANES), nt(sx[k], act2[...]))
 
     each(chunks, last_pass)
 
-    half = MID_ROWS // 2
-    out_ref[0:MID_ROWS, :] = g2[:, 0:LANES]
-    out_ref[HALF_BASE : HALF_BASE + half, 0:CH] = g2[0:half, LANES:]
-    out_ref[HALF_BASE : HALF_BASE + half, CH:LANES] = g2[half:, LANES:]
     both = [small[pl.ds(o, 27, stride=8), :] for o in range(6)]
     planes = [pair[:, 0:CH] for pair in both] + [pair[:, CH:LANES] for pair in both[0:3]]
     for n, plane in enumerate(planes):
@@ -658,29 +666,56 @@
     out_ref[MISC_BASE : MISC_BASE + 1, 0:CH] = line(grad_gain)
     out_ref[MISC_BASE : MISC_BASE + 1, CH:LANES] = line(grad_shift)
     out_ref[MISC_BASE + 1 : MISC_BASE + 2, :] = jnp.full((1, LANES), loss, F32)
-    devices = packed_ref.shape[0]
-    mid, rest, top, _ = shares(devices)
-    for d in range(devices):
-        own = out_ref[PLANE_BASE + d * rest : PLANE_BASE + (d + 1) * rest, :]
-        high, low = two_parts(own)
-        both = jnp.concatenate([out_ref[d * mid : (d + 1) * mid, :], own], axis=0)
-        packed_ref[d, 0:top, :] = fill(both, top).astype(BF16)
-        packed_ref[d, top:, :] = fill(low.astype(F32), packed_ref.shape[1] - top).astype(BF16)
+    sources = mine_ref.shape[0]
+    devices = 2 * sources
+    mid, rest, _, _ = shares(devices)
+    upper_band = lax.axis_index("band") == 1
+    for j in range(sources):
+        pair = []
+        for d in (2 * j, 2 * j + 1):
+            own = out_ref[PLANE_BASE + d * rest : PLANE_BASE + (d + 1) * rest, :]
+            pair.append(settled(out_ref[d * mid : (d + 1) * mid, :], own, devices))
+        mine_ref[j] = jnp.where(upper_band, pair[1], pair[0]).astype(BF16)
+        theirs_ref[j] = jnp.where(upper_band, pair[0], pair[1]).astype(BF16)
+
+
+def settled(middle, own, devices):
+    mid, rest, top, rows = shares(devices)
+    high, low = two_parts(own)
+    both = jnp.concatenate([middle, high.astype(F32)], axis=0)
+    return jnp.concatenate([fill(both, top), fill(low.astype(F32), rows - top)], axis=0)
+
+
+def pair_kernel(mine_ref, theirs_ref, out_ref):
+    sources = mine_ref.shape[0]
+    mid, rest, top, _ = shares(2 * sources)
+    for j in range(sources):
+        both = mine_ref[j].astype(F32) + theirs_ref[j].astype(F32)
+        own = both[mid : mid + rest] + both[top : top + rest]
+        out_ref[j] = settled(both[0:mid], own, 2 * sources).astype(BF16)
+
+
+def pair_sum(mine, theirs):
+    return pl.pallas_call(
+        pair_kernel,
+        out_shape=jax.ShapeDtypeStruct(mine.shape, BF16),
+        in_specs=[VMEM] * 2,
+        out_specs=VMEM,
+        compiler_params=small_params(4),
+        name="pair_sum",
+    )(mine, theirs)
 
 
 def combine_kernel(parts_ref, out_ref):
-    devices = parts_ref.shape[0]
-    mid, rest, top, rows = shares(devices)
+    sources = parts_ref.shape[0]
+    mid, rest, top, _ = shares(2 * sources)
     total = parts_ref[0].astype(F32)
-    for d in range(1, devices):
-        total = total + parts_ref[d].astype(F32)
+    for j in range(1, sources):
+        total = total + parts_ref[j].astype(F32)
     own = total[mid : mid + rest] + total[top : top + rest]
-    high, low = two_parts(own)
-    whole = jnp.concatenate(
-        [fill(jnp.concatenate([total[0:mid], own], axis=0), top), fill(low.astype(F32), rows - top)], axis=0
-    ).astype(BF16)
-    for d in range(devices):
-        out_ref[d] = whole
+    whole = settled(total[0:mid], own, 2 * sources).astype(BF16)
+    for j in range(sources):
+        out_ref[j] = whole
 
 
 def combine(parts):
@@ -699,12 +734,13 @@
     width = KIN * LANES
     return pl.pallas_call(
         functools.partial(train_kernel, factor),
-        out_shape=jax.ShapeDtypeStruct((devices, shares(devices)[3], LANES), BF16),
+        out_shape=(jax.ShapeDtypeStruct((devices // 2, shares(devices)[3], LANES), BF16),) * 2,
         in_specs=[SMEM] + [VMEM] * 8,
-        out_specs=VMEM,
+        out_specs=(VMEM,) * 2,
         scratch_shapes=[
             pltpu.VMEM((chunks, TAP_ROWS, width), BF16),
             pltpu.VMEM((chunks, CH, width), F32),
+            pltpu.VMEM((3 * CH, width), BF16),
             pltpu.VMEM((3 * CH, width), BF16),
             pltpu.VMEM((CH, width), F32),
             pltpu.VMEM((CH, width), BF16),
@@ -723,16 +759,23 @@
 
 
 def update_kernel(
-    whole_ref, wf_ref, gain_ref, shift_ref, wm_ref, wl_ref, nf_ref, ng_ref, ns_ref, nm_ref, nl_ref, loss_ref, grad_ref
+    mine_ref, theirs_ref, wf_ref, gain_ref, shift_ref, wm_ref, wl_ref,
+    nf_ref, ng_ref, ns_ref, nm_ref, nl_ref, loss_ref, grad_ref,
 ):
-    devices = whole_ref.shape[0]
-    mid, rest, top, _ = shares(devices)
-    for d in range(devices):
-        grad_ref[d * mid : (d + 1) * mid, :] = whole_ref[d, 0:top, :].astype(F32)[0:mid]
-    for d in range(devices):
-        high = whole_ref[d, 0:top, :].astype(F32)[mid : mid + rest]
-        low = whole_ref[d, top:, :].astype(F32)[0:rest]
-        grad_ref[PLANE_BASE + d * rest : PLANE_BASE + (d + 1) * rest, :] = high + low
+    sources = mine_ref.shape[0]
+    mid, rest, top, _ = shares(2 * sources)
+    upper_band = lax.axis_index("band") == 1
+    for j in range(sources):
+        mine, theirs = mine_ref[j].astype(F32), theirs_ref[j].astype(F32)
+        pair = (jnp.where(upper_band, theirs, mine), jnp.where(upper_band, mine, theirs))
+        for d, share in zip((2 * j, 2 * j + 1), pair):
+            grad_ref[d * mid : (d + 1) * mid, :] = share[0:mid]
+    for j in range(sources):
+        mine, theirs = mine_ref[j].astype(F32), theirs_ref[j].astype(F32)
+        pair = (jnp.where(upper_band, theirs, mine), jnp.where(upper_band, mine, theirs))
+        for d, share in zip((2 * j, 2 * j + 1), pair):
+            own = share[mid : mid + rest] + share[top : top + rest]
+            grad_ref[PLANE_BASE + d * rest : PLANE_BASE + (d + 1) * rest, :] = own
     half = MID_ROWS // 2
     fold = grad_ref[HALF_BASE : HALF_BASE + half, :]
     last = jnp.concatenate([fold[:, :CH], fold[:, CH:]], axis=0)
@@ -756,21 +799,25 @@
     loss_ref[...] = grad_ref[MISC_BASE + 1 : MISC_BASE + 2, 0:1]
 
 
-def update(whole, wf, gain, shift, wm, wl):
+def update(mine, theirs, wf, gain, shift, wm, wl):
     shapes = [wf, gain, shift, wm, wl]
     return pl.pallas_call(
         update_kernel,
         out_shape=tuple(jax.ShapeDtypeStruct(w.shape, F32) for w in shapes) + (jax.ShapeDtypeStruct((1, 1), F32),),
-        in_specs=[VMEM] * 6,
+        in_specs=[VMEM] * 7,
         out_specs=(VMEM,) * 6,
-        scratch_shapes=[pltpu.VMEM((padded_rows(whole.shape[0])[1], LANES), F32)],
+        scratch_shapes=[pltpu.VMEM((padded_rows(2 * mine.shape[0])[1], LANES), F32)],
         compiler_params=small_params(12),
         name="update",
-    )(whole, *shapes)
+    )(mine, theirs, *shapes)
 
 
 def exchange(rows):
-    return lax.all_to_all(rows, ("sec", "band"), split_axis=0, concat_axis=0, tiled=True)
+    return lax.all_to_all(rows, "sec", split_axis=0, concat_axis=0, tiled=True)
+
+
+def other_band(rows):
+    return lax.ppermute(rows, "band", [(0, 1), (1, 0)])
 
 
 def on_device(
@@ -787,7 +834,7 @@
     held, near, far, plane = edges_step(velocity)
     first = lax.ppermute(near, "sec", [(i, i ^ 1) for i in range(sources)])
     second = lax.ppermute(far, "sec", [(i, ((i + 1) ^ 1) - 1) for i in range(1, sources - 1)])
-    beyond = lax.ppermute(plane, "band", [(0, 1), (1, 0)])
+    beyond = other_band(plane)
 
     inner = inner_step(crop_level, crop_x, crop_y, held)
     edges = (near, far, plane, first, second, beyond)
@@ -799,9 +846,9 @@
     batch = batch.reshape(sources // CHUNK, LANES, KIN * FIELD_ROWS)
     factor = 1.0 / (6.0 * PZ * PX * PY * (groups * sources * 5 // 8))
     gain, shift = norm_gain.reshape(1, CH), norm_shift.reshape(1, CH)
-    parts = train(factor, groups, live_count, batch, gain, shift, weights)
-    whole = exchange(combine(exchange(parts)))
-    nf, ng, ns, nm, nl, loss = update(whole, wf, gain, shift, w_middle, wl)
+    mine, theirs = train(factor, groups, live_count, batch, gain, shift, weights)
+    mine = exchange(combine(exchange(pair_sum(mine, other_band(theirs)))))
+    nf, ng, ns, nm, nl, loss = update(mine, other_band(mine), wf, gain, shift, w_middle, wl)
     return (
         velocity_next,
         jnp.transpose(nf, (1, 2, 0)),

time: 62.3 us -> 59.4 us (0.953)
  blocking collectives: 27.8 us -> 22.2 us
  waiting for transfers between devices: 4.76 us -> 7.53 us
    all_to_all x2, blocking collectives: 27.8 us -> 22.2 us  [exchange(): return lax.all_to_all(rows, 'sec', split_axis=0, concat_axis=0, tiled=True)]
    ppermute x1 -> x3, waiting for transfers between devices: 0.01 us -> 2.78 us  [other_band(): return lax.ppermute(rows, 'band', [(0, 1), (1, 0)])]
    pallas_call x1 -> x2, Pallas kernels: 5.48 us -> 5.38 us  [the longest x1 5.32 us: train(): pl.pallas_call(functools.partial(train_kernel, factor), out_shape=(jax.Sh...]
  transfers between devices with their start and end apart: 4 -> 6, of which waited for: 1 -> 3; matrix products, arithmetic and copies ran while one was open for 0% -> 0% of each run, Pallas kernels for 7% -> 7%
where the time goes in v2:
time: 59.4 us; the launch traced here: 59.1 us
  blocking collectives  22.2 us (37%)
  Pallas kernels  13.7 us (23%)
  starting transfers between devices  12.8 us (22%)
  waiting for transfers between devices  7.53 us (13%)
  between operations  1.45 us (2%)
  local copies, waits for them, and re-layouts  1.44 us (2%)
    all_to_all x2, blocking collectives, exchange(): return lax.all_to_all(rows, 'sec', split_axis=0, concat_axis=0, tiled=True)  22.2 us
    all_to_all x1, starting transfers between devices, on_device(): lax.all_to_all(crops, 'sec', split_axis=0, concat_axis=0, tiled=True)  8.95 us
    pallas_call x1, Pallas kernels, train(): pl.pallas_call(functools.partial(train_kernel, factor), out_shape=(jax.Sh...  5.32 us
    all_to_all x1, waiting for transfers between devices, on_device(): lax.all_to_all(crops, 'sec', split_axis=0, concat_axis=0, tiled=True)  4.75 us
    ppermute x1, starting transfers between devices, on_device(): first = lax.ppermute(near, 'sec', [(i, i ^ 1) for i in range(sources)])  3.03 us
    ppermute x3, waiting for transfers between devices, other_band(): return lax.ppermute(rows, 'band', [(0, 1), (1, 0)])  2.78 us
    pallas_call x1, Pallas kernels, inner_step(): pl.pallas_call(inner_kernel, out_shape=(jax.ShapeDtypeStruct(velocity.sha...  2.58 us
    pallas_call x1, Pallas kernels, edges_step(): pl.pallas_call(edges_kernel, out_shape=(jax.ShapeDtypeStruct(velocity.sha...  1.66 us
  transfers between devices with their start and end apart: 6, of which 3 were waited for; matrix products, arithmetic and copies ran while one was open for 0% of the time, Pallas kernels for 7%

profile of v2, /device:TPU:0, one launch (start us, length us, event | category | flops | bytes accessed | tf_op | source)
XLA Modules:
  0.0 59.1 jit_solution(12289854068580037633)
XLA Ops:
  0.6 1.7 %edges_step.1 = (f32[3,16,16,512]{3,2,1,0:T(8,128)S(1)}, f32[3,16,512]{2,1,0:T(8,128)S(1)}, f32[3,16,512]{2,1,0:T(8,128)S(1)}, f32[3,16,512]{2,1,0:T(8,128)S(1)}) custom-call(f32[3,16,16,512]{3,2,1,0:T(8,128)} %source_ref.1), custom_call_target="tpu_custom_call" | custom-call | flops 1000000 | bytes 3000000 | tf_op jit(solution)/shard_map/edges_step/pallas_call | solution.py:187
  2.3 3.0 %collective-permute-start = (f32[3,16,512]{2,1,0:T(8,128)S(1)}, f32[3,16,512]{2,1,0:T(8,128)S(1)}, u32[]{:S(2)}, u32[]{:S(2)}) collective-permute-start(f32[3,16,512]{2,1,0:T(8,128)S(1)} %get-tuple-element.36.near_ref), channel_id=1, source_target_pairs={{0,2},{2,0},{4,6},{6,4},{8,10},{10,8},{12,14},{14,12},{16,18},{18,... | collective-permute-start | bytes 294920 | tf_op jit(solution)/shard_map/ppermute | solution.py:835
  5.3 0.7 %collective-permute-start.1 = (f32[3,16,512]{2,1,0:T(8,128)S(1)}, f32[3,16,512]{2,1,0:T(8,128)S(1)}, u32[]{:S(2)}, u32[]{:S(2)}) collective-permute-start(f32[3,16,512]{2,1,0:T(8,128)S(1)} %get-tuple-element.37.far_ref), channel_id=1, source_target_pairs={{2,4},{4,2},{6,8},{8,6},{10,12},{12,10},{14,16},{16,14},{18,20},{2... | collective-permute-start | bytes 294920 | tf_op jit(solution)/shard_map/ppermute | solution.py:836
  6.0 0.1 collective-permute-start.2
  6.1 0.0 copy-start
  6.1 0.0 copy-start.1
  6.1 0.0 copy-start.2
  6.1 2.6 %inner_step.1 = (f32[3,16,16,512]{3,2,1,0:T(8,128)S(1)}, f32[1,4,3,8,256]{4,3,2,1,0:T(8,128)S(1)}, bf16[1,512,256]{2,1,0:T(8,128)(2,1)S(1)}, bf16[288,256]{1,0:T(8,128)(2,1)S(1)}, s32[1,8,256]{2,1,0:T(8,128)S(1)}) custom-call(s32[1,16]{1,0:T(1,128)} %bitcast.25, s32[1,16]{1,0:T(1,128)} %bitcast.26, s32[1,16]{1,0:T(1,128)} %bitcast.27, ...), custom_call_target="tpu_custom_call" | custom-call | flops 3000000000 | bytes 8000000 | tf_op jit(solution)/shard_map/inner_step/pallas_call | solution.py:376
  8.7 0.0 copy-start.5
  9.4 0.0 copy-done
  9.4 0.0 copy-done.1
  9.4 0.0 copy-done.2
  9.4 0.3 arrange_weights.1
  9.7 0.0 collective-permute-done.first_ref
  9.7 0.0 collective-permute-done.1.second_ref
  9.7 0.0 collective-permute-done.2.beyond_ref
  9.7 1.3 %cut_crops.1 = bf16[1,128,256]{2,1,0:T(8,128)(2,1)} custom-call(s32[1,8,256]{2,1,0:T(8,128)S(1)} %get-tuple-element.32.where_ref, f32[1,4,3,8,256]{4,3,2,1,0:T(8,128)S(1)} %get-tuple-element.33.cells_ref, bf16[1,512,256]{2,1,0:T(8,128)(2,1)S(1)} %get-tuple-element.34.picks_ref, bf16[288,256]{1,0:T(8,128)(2,1)S(1)} %get-tuple-element.35.goal_ref, ...), custom_call_target="tpu_custom_call" | custom-call | flops 1000000000 | bytes 3000000 | tf_op jit(solution)/shard_map/cut_crops/pallas_call | solution.py:402
  11.0 0.0 copy-done.5
  11.0 9.0 %all-to-all-start = ((bf16[16,8,256]{2,1,0:T(8,128)(2,1)}), bf16[16,8,256]{2,1,0:T(8,128)(2,1)S(1)}, u32[]{:S(2)}, u32[]{:S(2)}) async-start(bf16[16,8,256]{2,1,0:T(8,128)(2,1)} %bitcast.3), calls=%async_computation | async-start | bytes 131072 | tf_op jit(solution)/shard_map/all_to_all | solution.py:844
  19.9 0.0 copy-start.6
  20.0 1.4 %copy-done.6 = f32[3,16,16,512]{3,2,1,0:T(8,128)S(1)} copy-done((f32[3,16,16,512]{3,2,1,0:T(8,128)S(1)}, f32[3,16,16,512]{3,2,1,0:T(8,128)}, u32[]{:S(2)}) %copy-start.6) | copy-done | bytes 1572888
  21.4 0.0 copy-start.3
  21.4 0.0 copy-start.4
  21.4 1.4 %finish_step.1 = f32[3,16,16,512]{3,2,1,0:T(8,128)} custom-call(f32[3,16,16,512]{3,2,1,0:T(8,128)S(1)} %copy-done.6, f32[3,16,512]{2,1,0:T(8,128)S(1)} %get-tuple-element.36.near_ref, f32[3,16,512]{2,1,0:T(8,128)S(1)} %get-tuple-element.37.far_ref, f32[3,16,512]{2,1,0:T(8,128)S(1)} %get-tuple-element.38.plane_ref, ...), custom_call_target="tpu_custom_call" | custom-call | flops 2000000000 | bytes 4000000 | tf_op jit(solution)/shard_map/finish_step/pallas_call | solution.py:415
  22.7 4.8 %all-to-all-done = bf16[16,8,256]{2,1,0:T(8,128)(2,1)S(1)} async-done(((bf16[16,8,256]{2,1,0:T(8,128)(2,1)}), bf16[16,8,256]{2,1,0:T(8,128)(2,1)S(1)}, u32[]{:S(2)}, u32[]{:S(2)}) %all-to-all-start) | async-done | bytes 65568 | tf_op jit(solution)/shard_map/all_to_all | solution.py:844
  27.5 0.0 copy-done.3
  27.5 0.0 copy-done.4
  27.5 5.3 %train_step.1 = (bf16[16,40,128]{2,1,0:T(8,128)(2,1)S(1)}, bf16[16,40,128]{2,1,0:T(8,128)(2,1)S(1)}) custom-call(s32[1]{0:T(128)S(6)} %copy.17.count_ref, bf16[1,128,256]{2,1,0:T(8,128)(2,1)S(1)} %bitcast.16, f32[1,64]{1,0:T(1,128)S(1)} %bitcast.19, f32[1,64]{1,0:T(1,128)S(1)} %bitcast.21, bf16[64,216]{1,0:T(8,128)(2,1)S(1)} %get-tuple-element.42.w1_ref, ...), custom_call_target="tpu_custom_call" | custom-call | tf_op jit(solution)/shard_map/train_step/pallas_call | solution.py:735
  32.8 0.1 collective-permute-start.3
  32.9 1.4 %collective-permute-done.3.theirs_ref = bf16[16,40,128]{2,1,0:T(8,128)(2,1)S(1)} collective-permute-done((bf16[16,40,128]{2,1,0:T(8,128)(2,1)S(1)}, bf16[16,40,128]{2,1,0:T(8,128)(2,1)S(1)}, u32[]{:S(2)}, u32[]{:S(2)}) %collective-permute-start.3) | collective-permute-done | bytes 163872 | tf_op jit(solution)/shard_map/ppermute | solution.py:820
  34.3 0.1 pair_sum.1
  34.3 11.0 %all_to_all.15.parts_ref = bf16[16,40,128]{2,1,0:T(8,128)(2,1)S(1)} all-to-all(bf16[16,40,128]{2,1,0:T(8,128)(2,1)S(1)} %pair_sum.1), channel_id=1, replica_groups=mesh['sec'=16,'band'=2] {'sec'}, dimensions={0} | all-to-all | bytes 327680 | tf_op jit(solution)/shard_map/all_to_all | solution.py:816
  45.4 11.1 %all_to_all.16.mine_ref = bf16[16,40,128]{2,1,0:T(8,128)(2,1)S(1)} all-to-all(bf16[16,40,128]{2,1,0:T(8,128)(2,1)S(1)} %combine.1), channel_id=1, replica_groups=mesh['sec'=16,'band'=2] {'sec'}, dimensions={0} | all-to-all | bytes 327680 | tf_op jit(solution)/shard_map/all_to_all | solution.py:816
  56.5 0.0 collective-permute-start.4
  56.5 1.4 %collective-permute-done.4.theirs_ref = bf16[16,40,128]{2,1,0:T(8,128)(2,1)S(1)} collective-permute-done((bf16[16,40,128]{2,1,0:T(8,128)(2,1)S(1)}, bf16[16,40,128]{2,1,0:T(8,128)(2,1)S(1)}, u32[]{:S(2)}, u32[]{:S(2)}) %collective-permute-start.4) | collective-permute-done | bytes 163872 | tf_op jit(solution)/shard_map/ppermute | solution.py:820
  57.9 1.1 %update.1 = (f32[3,27,64]{2,1,0:T(8,128)}, f32[1,64]{1,0:T(1,128)}, f32[1,64]{1,0:T(1,128)}, f32[27,64,64]{2,1,0:T(8,128)}, f32[6,27,64]{2,1,0:T(8,128)}, /*index=5*/f32[1,1]{1,0:T(1,128)}) custom-call(bf16[16,40,128]{2,1,0:T(8,128)(2,1)S(1)} %all_to_all.16.mine_ref, bf16[16,40,128]{2,1,0:T(8,128)(2,1)S(1)} %collective-permute-done.4.theirs_ref, ...), custom_call_target="tpu_custom_call" | custom-call | tf_op jit(solution)/shard_map/update/pallas_call | solution.py:804
  (1 shorter events, 0.0 us)
Async XLA Ops:
  2.3 7.4 %collective-permute-start = (f32[3,16,512]{2,1,0:T(8,128)S(1)}, f32[3,16,512]{2,1,0:T(8,128)S(1)}, u32[]{:S(2)}, u32[]{:S(2)}) collective-permute-start(f32[3,16,512]{2,1,0:T(8,128)S(1)} %get-tuple-element.36.near_ref), channel_id=1, source_target_pairs={{0,2},{2,0},{4,6},{6,4},{8,10},{10,8},{12,14},{14,12},{16,18},{18,... | collective-permute-start | bytes 294920 | tf_op jit(solution)/shard_map/ppermute | solution.py:835
  5.3 4.4 %collective-permute-start.1 = (f32[3,16,512]{2,1,0:T(8,128)S(1)}, f32[3,16,512]{2,1,0:T(8,128)S(1)}, u32[]{:S(2)}, u32[]{:S(2)}) collective-permute-start(f32[3,16,512]{2,1,0:T(8,128)S(1)} %get-tuple-element.37.far_ref), channel_id=1, source_target_pairs={{2,4},{4,2},{6,8},{8,6},{10,12},{12,10},{14,16},{16,14},{18,20},{2... | collective-permute-start | bytes 294920 | tf_op jit(solution)/shard_map/ppermute | solution.py:836
  6.0 3.7 %collective-permute-start.2 = (f32[3,16,512]{2,1,0:T(8,128)S(1)}, f32[3,16,512]{2,1,0:T(8,128)S(1)}, u32[]{:S(2)}, u32[]{:S(2)}) collective-permute-start(f32[3,16,512]{2,1,0:T(8,128)S(1)} %get-tuple-element.38.plane_ref), channel_id=1, source_target_pairs={{0,1},{1,0},{2,3},{3,2},{4,5},{5,4},{6,7},{7,6},{8,9},{9,8},{10,11... | collective-permute-start | bytes 294920 | tf_op jit(solution)/shard_map/ppermute | solution.py:820
  6.1 3.3 %copy-start = (f32[27,64,64]{2,1,0:T(8,128)S(1)}, f32[27,64,64]{2,1,0:T(8,128)}, u32[]{:S(2)}) copy-start(f32[27,64,64]{2,1,0:T(8,128)} %wm_ref.3) | copy-start | bytes 1327108
  6.1 3.3 %copy-start.1 = (f32[27,6,64]{2,0,1:T(8,128)S(1)}, f32[27,6,64]{2,0,1:T(8,128)}, u32[]{:S(2)}) copy-start(f32[27,6,64]{2,0,1:T(8,128)} %param.19) | copy-start | bytes 124420
  6.1 3.3 %copy-start.2 = (f32[27,64,3]{1,0,2:T(8,128)S(1)}, f32[27,64,3]{1,0,2:T(8,128)}, u32[]{:S(2)}) copy-start(f32[27,64,3]{1,0,2:T(8,128)} %param.15) | copy-start | bytes 62212
  8.7 2.3 %copy-start.5 = (f32[3,16,16,512]{3,2,1,0:T(8,128)}, f32[3,16,16,512]{3,2,1,0:T(8,128)S(1)}, u32[]{:S(2)}) copy-start(f32[3,16,16,512]{3,2,1,0:T(8,128)S(1)} %get-tuple-element.39.vn_ref) | copy-start | bytes 4718596
  11.0 16.5 %all-to-all-start = ((bf16[16,8,256]{2,1,0:T(8,128)(2,1)}), bf16[16,8,256]{2,1,0:T(8,128)(2,1)S(1)}, u32[]{:S(2)}, u32[]{:S(2)}) async-start(bf16[16,8,256]{2,1,0:T(8,128)(2,1)} %bitcast.3), calls=%async_computation | async-start | bytes 131072 | tf_op jit(solution)/shard_map/all_to_all | solution.py:844
  19.9 1.4 %copy-start.6 = (f32[3,16,16,512]{3,2,1,0:T(8,128)S(1)}, f32[3,16,16,512]{3,2,1,0:T(8,128)}, u32[]{:S(2)}) copy-start(f32[3,16,16,512]{3,2,1,0:T(8,128)} %copy-done.5) | copy-start | bytes 4718596
  21.4 6.1 %copy-start.3 = (f32[64]{0:T(128)S(1)}, f32[64]{0:T(128)}, u32[]{:S(2)}) copy-start(f32[64]{0:T(128)} %param.16) | copy-start | bytes 772
  21.4 6.1 %copy-start.4 = (f32[64]{0:T(128)S(1)}, f32[64]{0:T(128)}, u32[]{:S(2)}) copy-start(f32[64]{0:T(128)} %param.17) | copy-start | bytes 772
  32.8 1.5 %collective-permute-start.3 = (bf16[16,40,128]{2,1,0:T(8,128)(2,1)S(1)}, bf16[16,40,128]{2,1,0:T(8,128)(2,1)S(1)}, u32[]{:S(2)}, u32[]{:S(2)}) collective-permute-start(bf16[16,40,128]{2,1,0:T(8,128)(2,1)S(1)} %get-tuple-element.48), channel_id=1, source_target_pairs={{0,1},{1,0},{2,3},{3,2},{4,5},{5,4},{6,7},{7,6},{8,9},{9,8},{10,11... | collective-permute-start | bytes 491528 | tf_op jit(solution)/shard_map/ppermute | solution.py:820
  56.5 1.4 %collective-permute-start.4 = (bf16[16,40,128]{2,1,0:T(8,128)(2,1)S(1)}, bf16[16,40,128]{2,1,0:T(8,128)(2,1)S(1)}, u32[]{:S(2)}, u32[]{:S(2)}) collective-permute-start(bf16[16,40,128]{2,1,0:T(8,128)(2,1)S(1)} %all_to_all.16.mine_ref), channel_id=1, source_target_pairs={{0,1},{1,0},{2,3},{3,2},{4,5},{5,4},{6,7},{7,6},{8,9},{9,8},{10,11... | collective-permute-start | bytes 491528 | tf_op jit(solution)/shard_map/ppermute | solution.py:820

commit v3 on v2

--- a/solution.py
+++ b/solution.py
@@ -84,7 +84,7 @@
         lax.fori_loop(0, number, lambda i, c: (body(i), c)[1], 0)
 
 
-def weights_kernel(wf_ref, wm_ref, wl_ref, w1_ref, w2f_ref, w2b_ref, w3f_ref, w3b_ref, rows):
+def weights_kernel(wf_ref, wm_ref, wl_ref, w1_ref, w2f_ref, w2b_ref, w3f_ref, w3b_ref, goal_ref, rows):
     rows[...] = jnp.zeros_like(rows)
     for c in range(3):
         rows[pl.ds(c, 27, stride=8), :] = wf_ref[c]
@@ -99,6 +99,13 @@
         rows_at = slice(zx * CH, (zx + 1) * CH)
         w2f_ref[rows_at, :] = jnp.concatenate(taps, axis=1).astype(BF16)
         w2b_ref[rows_at, :] = jnp.transpose(jnp.concatenate(taps, axis=0)).astype(BF16)
+    ch_rows = 9 * PZ * 8
+    r = lax.broadcasted_iota(jnp.int32, (ch_rows, KIN * FIELD_ROWS), 0)
+    col = lax.broadcasted_iota(jnp.int32, (ch_rows, KIN * FIELD_ROWS), 1)
+    channel = r >> 5
+    slot = jnp.where(channel < 3, channel, channel + 5)
+    goal = ((((r >> 3) & 3) * PX + ((r & 7) >> 1)) * FIELD_ROWS) + slot
+    goal_ref[...] = jnp.where((col == goal) & ((r & 1) == 0), 1.0, 0.0).astype(BF16)
 
 
 def arrange_weights(wf, wm, wl):
@@ -110,9 +117,10 @@
             jax.ShapeDtypeStruct((9 * CH, 3 * CH), BF16),
             jax.ShapeDtypeStruct((TAP_ROWS, CH), BF16),
             jax.ShapeDtypeStruct((CH, TAP_ROWS), BF16),
+            jax.ShapeDtypeStruct((9 * PZ * 8, KIN * FIELD_ROWS), BF16),
         ),
         in_specs=[VMEM] * 3,
-        out_specs=(VMEM,) * 5,
+        out_specs=(VMEM,) * 6,
         scratch_shapes=[pltpu.VMEM((TAP_ROWS, CH), F32)],
         compiler_params=small_params(6),
         name="arrange_weights",
@@ -162,14 +170,17 @@
     odd = lax.axis_index("sec") % 2 == 1
     upper_band = lax.axis_index("band") == 1
     _, levels, nx, ny = v_ref.shape
-    arrivals = [
-        pltpu.make_async_copy(source_ref.at[:, l], v_ref.at[:, l], loads.at[l]) for l in range(levels)
-    ]
+    pieces = loads.shape[0] // 3
+    span = levels // pieces
+    arrivals = []
+    for n in range(3 * pieces):
+        where = (n // pieces, pl.ds(n % pieces * span, span))
+        arrivals.append(pltpu.make_async_copy(source_ref.at[where], v_ref.at[where], loads.at[n]))
     for arrival in arrivals:
         arrival.start()
-    for arrival in arrivals:
-        arrival.wait()
     for c in range(3):
+        for arrival in arrivals[c * pieces : (c + 1) * pieces]:
+            arrival.wait()
         head = v_ref[c, :, 0, :]
         tail = v_ref[c, :, nx - 1, :]
         near_ref[c] = jnp.where(odd, head, tail)
@@ -191,7 +202,7 @@
         ),
         in_specs=[HBM],
         out_specs=(VMEM,) * 4,
-        scratch_shapes=[pltpu.SemaphoreType.DMA((levels,))],
+        scratch_shapes=[pltpu.SemaphoreType.DMA((12,))],
         compiler_params=small_params(6),
         cost_estimate=cost(10**6, 3 * 10**6),
         name="edges_step",
@@ -199,7 +210,7 @@
 
 
 def inner_kernel(
-    level_ref, cx_ref, cy_ref, v_ref, vn_ref, cells_ref, picks_ref, goal_ref, where_ref, parts, chosen, spots, sems
+    level_ref, cx_ref, cy_ref, v_ref, vn_ref, cells_ref, picks_ref, where_ref, parts, chosen, spots, sems
 ):
     _, levels, nx, ny = v_ref.shape
     chunks = cells_ref.shape[0]
@@ -257,13 +268,6 @@
                 cells_ref[k, l, c] = x_window(kept[l], x_of)
 
     each(chunks, chunk)
-    ch_rows = 9 * PZ * 8
-    r = lax.broadcasted_iota(jnp.int32, (ch_rows, KIN * FIELD_ROWS), 0)
-    col = lax.broadcasted_iota(jnp.int32, (ch_rows, KIN * FIELD_ROWS), 1)
-    channel = r >> 5
-    slot = jnp.where(channel < 3, channel, channel + 5)
-    goal = ((((r >> 3) & 3) * PX + ((r & 7) >> 1)) * FIELD_ROWS) + slot
-    goal_ref[...] = jnp.where((col == goal) & ((r & 1) == 0), 1.0, 0.0).astype(BF16)
 
 
 def beyond_terms(near_ref, far_ref, plane_ref, first_ref, second_ref, beyond_ref):
@@ -379,11 +383,10 @@
             jax.ShapeDtypeStruct(velocity.shape, F32),
             jax.ShapeDtypeStruct((chunks, PZ, 3, 2 * PX, 2 * LANES), F32),
             jax.ShapeDtypeStruct((chunks, ny, 2 * LANES), BF16),
-            jax.ShapeDtypeStruct((9 * PZ * 8, KIN * FIELD_ROWS), BF16),
             jax.ShapeDtypeStruct((chunks, 8, 2 * LANES), jnp.int32),
         ),
         in_specs=[HBM, HBM, HBM, VMEM],
-        out_specs=(VMEM,) * 5,
+        out_specs=(VMEM,) * 4,
         scratch_shapes=[
             pltpu.VMEM((levels * 9 * nx, ny), BF16),
             pltpu.VMEM((levels, 3 * nx, 2 * LANES), F32),
@@ -396,8 +399,8 @@
     )(*[in_hbm(x.reshape(1, samples)) for x in (level, cx, cy)], velocity)
 
 
-def cut_crops(inner, edges):
-    _, cells, picks, goal, where = inner
+def cut_crops(inner, goal, edges):
+    _, cells, picks, where = inner
     chunks = cells.shape[0]
     return pl.pallas_call(
         crop_kernel,
@@ -592,7 +595,6 @@
             des[:, where] = value
 
         stack_taps(errors, -1, store)
-        add_to(small, slice(0, CH), nt(des[...], act2[...]))
         for l in range(PZ):
             got = mm(w3b_ref[...], des[:, l * band : (l + 1) * band])
             for x in range(PX):
@@ -615,6 +617,7 @@
                         dys[n * CH : (n + 1) * CH, at(l, x)] = zero
         plane_products(w2b_ref, s3, -1, act_cot)
         add_to(g2, slice(None), nt(dys[...], s2[...]))
+        add_to(small, slice(0, CH), nt(des[...], act2[...]))
         by_gain = flat[:, 0:LANES]
         by_shift = flat[:, LANES : 2 * LANES]
         for b in range(KIN):
@@ -838,7 +841,7 @@
 
     inner = inner_step(crop_level, crop_x, crop_y, held)
     edges = (near, far, plane, first, second, beyond)
-    crops = cut_crops(inner, edges)
+    crops = cut_crops(inner, weights[-1], edges)
     velocity_next = finish_step(inner, edges)
     crops = crops.reshape(sources, PY, KIN * FIELD_ROWS)
     batch = lax.all_to_all(crops, "sec", split_axis=0, concat_axis=0, tiled=True)
@@ -846,7 +849,7 @@
     batch = batch.reshape(sources // CHUNK, LANES, KIN * FIELD_ROWS)
     factor = 1.0 / (6.0 * PZ * PX * PY * (groups * sources * 5 // 8))
     gain, shift = norm_gain.reshape(1, CH), norm_shift.reshape(1, CH)
-    mine, theirs = train(factor, groups, live_count, batch, gain, shift, weights)
+    mine, theirs = train(factor, groups, live_count, batch, gain, shift, weights[:-1])
     mine = exchange(combine(exchange(pair_sum(mine, other_band(theirs)))))
     nf, ng, ns, nm, nl, loss = update(mine, other_band(mine), wf, gain, shift, w_middle, wl)
     return (

time: 59.4 us -> 59.1 us (level)
  no operation moved by 1% of the time
where the time goes in v3:
time: 59.1 us; the launch traced here: 58.8 us
  blocking collectives  22.2 us (38%)
  Pallas kernels  13.4 us (23%)
  starting transfers between devices  12.8 us (22%)
  waiting for transfers between devices  7.53 us (13%)
  between operations  1.45 us (2%)
  local copies, waits for them, and re-layouts  1.44 us (2%)
    all_to_all x2, blocking collectives, exchange(): return lax.all_to_all(rows, 'sec', split_axis=0, concat_axis=0, tiled=True)  22.2 us
    all_to_all x1, starting transfers between devices, on_device(): lax.all_to_all(crops, 'sec', split_axis=0, concat_axis=0, tiled=True)  8.98 us
    pallas_call x1, Pallas kernels, train(): pl.pallas_call(functools.partial(train_kernel, factor), out_shape=(jax.Sh...  5.11 us
    all_to_all x1, waiting for transfers between devices, on_device(): lax.all_to_all(crops, 'sec', split_axis=0, concat_axis=0, tiled=True)  4.75 us
    ppermute x1, starting transfers between devices, on_device(): first = lax.ppermute(near, 'sec', [(i, i ^ 1) for i in range(sources)])  3.03 us
    ppermute x3, waiting for transfers between devices, other_band(): return lax.ppermute(rows, 'band', [(0, 1), (1, 0)])  2.78 us
    pallas_call x1, Pallas kernels, inner_step(): pl.pallas_call(inner_kernel, out_shape=(jax.ShapeDtypeStruct(velocity.sha...  2.45 us
    pallas_call x1, Pallas kernels, edges_step(): pl.pallas_call(edges_kernel, out_shape=(jax.ShapeDtypeStruct(velocity.sha...  1.57 us
  transfers between devices with their start and end apart: 6, of which 3 were waited for; matrix products, arithmetic and copies ran while one was open for 0% of the time, Pallas kernels for 7%

profile of v3, /device:TPU:0, one launch (start us, length us, event | category | flops | bytes accessed | tf_op | source)
XLA Modules:
  0.0 58.8 jit_solution(14519014004955781715)
XLA Ops:
  0.6 1.6 %edges_step.1 = (f32[3,16,16,512]{3,2,1,0:T(8,128)S(1)}, f32[3,16,512]{2,1,0:T(8,128)S(1)}, f32[3,16,512]{2,1,0:T(8,128)S(1)}, f32[3,16,512]{2,1,0:T(8,128)S(1)}) custom-call(f32[3,16,16,512]{3,2,1,0:T(8,128)} %source_ref.1), custom_call_target="tpu_custom_call" | custom-call | flops 1000000 | bytes 3000000 | tf_op jit(solution)/shard_map/edges_step/pallas_call | solution.py:198
  2.2 3.0 %collective-permute-start = (f32[3,16,512]{2,1,0:T(8,128)S(1)}, f32[3,16,512]{2,1,0:T(8,128)S(1)}, u32[]{:S(2)}, u32[]{:S(2)}) collective-permute-start(f32[3,16,512]{2,1,0:T(8,128)S(1)} %get-tuple-element.36.near_ref), channel_id=1, source_target_pairs={{0,2},{2,0},{4,6},{6,4},{8,10},{10,8},{12,14},{14,12},{16,18},{18,... | collective-permute-start | bytes 294920 | tf_op jit(solution)/shard_map/ppermute | solution.py:838
  5.2 0.7 %collective-permute-start.1 = (f32[3,16,512]{2,1,0:T(8,128)S(1)}, f32[3,16,512]{2,1,0:T(8,128)S(1)}, u32[]{:S(2)}, u32[]{:S(2)}) collective-permute-start(f32[3,16,512]{2,1,0:T(8,128)S(1)} %get-tuple-element.37.far_ref), channel_id=1, source_target_pairs={{2,4},{4,2},{6,8},{8,6},{10,12},{12,10},{14,16},{16,14},{18,20},{2... | collective-permute-start | bytes 294920 | tf_op jit(solution)/shard_map/ppermute | solution.py:839
  5.9 0.1 collective-permute-start.2
  6.0 0.0 copy-start
  6.0 0.0 copy-start.1
  6.0 0.0 copy-start.2
  6.0 2.4 %inner_step.1 = (f32[3,16,16,512]{3,2,1,0:T(8,128)S(1)}, f32[1,4,3,8,256]{4,3,2,1,0:T(8,128)S(1)}, bf16[1,512,256]{2,1,0:T(8,128)(2,1)S(1)}, s32[1,8,256]{2,1,0:T(8,128)S(1)}) custom-call(s32[1,16]{1,0:T(1,128)} %bitcast.25, s32[1,16]{1,0:T(1,128)} %bitcast.26, s32[1,16]{1,0:T(1,128)} %bitcast.27, f32[3,16,16,512]{3,2,1,0:T(8,128)S(1)} %get-tuple-element.31.v_ref), custom_call_target="tpu_custom_call" | custom-call | flops 3000000000 | bytes 8000000 | tf_op jit(solution)/shard_map/inner_step/pallas_call | solution.py:380
  8.5 0.0 copy-start.5
  9.1 0.0 copy-done
  9.1 0.0 copy-done.1
  9.2 0.0 copy-done.2
  9.2 0.4 arrange_weights.1
  9.6 0.0 collective-permute-done.first_ref
  9.6 0.0 collective-permute-done.1.second_ref
  9.6 0.0 collective-permute-done.2.beyond_ref
  9.6 1.3 %cut_crops.1 = bf16[1,128,256]{2,1,0:T(8,128)(2,1)} custom-call(s32[1,8,256]{2,1,0:T(8,128)S(1)} %get-tuple-element.32.where_ref, f32[1,4,3,8,256]{4,3,2,1,0:T(8,128)S(1)} %get-tuple-element.33.cells_ref, bf16[1,512,256]{2,1,0:T(8,128)(2,1)S(1)} %get-tuple-element.34.picks_ref, bf16[288,256]{1,0:T(8,128)(2,1)S(1)} %get-tuple-element.35.goal_ref, ...), custom_call_target="tpu_custom_call" | custom-call | flops 1000000000 | bytes 3000000 | tf_op jit(solution)/shard_map/cut_crops/pallas_call | solution.py:405
  10.9 0.0 copy-done.5
  10.9 9.0 %all-to-all-start = ((bf16[16,8,256]{2,1,0:T(8,128)(2,1)}), bf16[16,8,256]{2,1,0:T(8,128)(2,1)S(1)}, u32[]{:S(2)}, u32[]{:S(2)}) async-start(bf16[16,8,256]{2,1,0:T(8,128)(2,1)} %bitcast.5), calls=%async_computation | async-start | bytes 131072 | tf_op jit(solution)/shard_map/all_to_all | solution.py:847
  19.9 0.0 copy-start.6
  19.9 1.4 %copy-done.6 = f32[3,16,16,512]{3,2,1,0:T(8,128)S(1)} copy-done((f32[3,16,16,512]{3,2,1,0:T(8,128)S(1)}, f32[3,16,16,512]{3,2,1,0:T(8,128)}, u32[]{:S(2)}) %copy-start.6) | copy-done | bytes 1572888
  21.3 0.0 copy-start.3
  21.3 0.0 copy-start.4
  21.3 1.4 %finish_step.1 = f32[3,16,16,512]{3,2,1,0:T(8,128)} custom-call(f32[3,16,16,512]{3,2,1,0:T(8,128)S(1)} %copy-done.6, f32[3,16,512]{2,1,0:T(8,128)S(1)} %get-tuple-element.36.near_ref, f32[3,16,512]{2,1,0:T(8,128)S(1)} %get-tuple-element.37.far_ref, f32[3,16,512]{2,1,0:T(8,128)S(1)} %get-tuple-element.38.plane_ref, ...), custom_call_target="tpu_custom_call" | custom-call | flops 2000000000 | bytes 4000000 | tf_op jit(solution)/shard_map/finish_step/pallas_call | solution.py:418
  22.6 4.8 %all-to-all-done = bf16[16,8,256]{2,1,0:T(8,128)(2,1)S(1)} async-done(((bf16[16,8,256]{2,1,0:T(8,128)(2,1)}), bf16[16,8,256]{2,1,0:T(8,128)(2,1)S(1)}, u32[]{:S(2)}, u32[]{:S(2)}) %all-to-all-start) | async-done | bytes 65568 | tf_op jit(solution)/shard_map/all_to_all | solution.py:847
  27.4 0.0 copy-done.3
  27.4 0.0 copy-done.4
  27.4 5.1 %train_step.1 = (bf16[16,40,128]{2,1,0:T(8,128)(2,1)S(1)}, bf16[16,40,128]{2,1,0:T(8,128)(2,1)S(1)}) custom-call(s32[1]{0:T(128)S(6)} %copy.17.count_ref, bf16[1,128,256]{2,1,0:T(8,128)(2,1)S(1)} %bitcast.16, f32[1,64]{1,0:T(1,128)S(1)} %bitcast.19, f32[1,64]{1,0:T(1,128)S(1)} %bitcast.21, bf16[64,216]{1,0:T(8,128)(2,1)S(1)} %get-tuple-element.42.w1_ref, ...), custom_call_target="tpu_custom_call" | custom-call | tf_op jit(solution)/shard_map/train_step/pallas_call | solution.py:738
  32.5 0.1 collective-permute-start.3
  32.6 1.4 %collective-permute-done.3.theirs_ref = bf16[16,40,128]{2,1,0:T(8,128)(2,1)S(1)} collective-permute-done((bf16[16,40,128]{2,1,0:T(8,128)(2,1)S(1)}, bf16[16,40,128]{2,1,0:T(8,128)(2,1)S(1)}, u32[]{:S(2)}, u32[]{:S(2)}) %collective-permute-start.3) | collective-permute-done | bytes 163872 | tf_op jit(solution)/shard_map/ppermute | solution.py:823
  34.0 0.1 pair_sum.1
  34.0 11.0 %all_to_all.15.parts_ref = bf16[16,40,128]{2,1,0:T(8,128)(2,1)S(1)} all-to-all(bf16[16,40,128]{2,1,0:T(8,128)(2,1)S(1)} %pair_sum.1), channel_id=1, replica_groups=mesh['sec'=16,'band'=2] {'sec'}, dimensions={0} | all-to-all | bytes 327680 | tf_op jit(solution)/shard_map/all_to_all | solution.py:819
  45.1 11.1 %all_to_all.16.mine_ref = bf16[16,40,128]{2,1,0:T(8,128)(2,1)S(1)} all-to-all(bf16[16,40,128]{2,1,0:T(8,128)(2,1)S(1)} %combine.1), channel_id=1, replica_groups=mesh['sec'=16,'band'=2] {'sec'}, dimensions={0} | all-to-all | bytes 327680 | tf_op jit(solution)/shard_map/all_to_all | solution.py:819
  56.2 0.0 collective-permute-start.4
  56.2 1.4 %collective-permute-done.4.theirs_ref = bf16[16,40,128]{2,1,0:T(8,128)(2,1)S(1)} collective-permute-done((bf16[16,40,128]{2,1,0:T(8,128)(2,1)S(1)}, bf16[16,40,128]{2,1,0:T(8,128)(2,1)S(1)}, u32[]{:S(2)}, u32[]{:S(2)}) %collective-permute-start.4) | collective-permute-done | bytes 163872 | tf_op jit(solution)/shard_map/ppermute | solution.py:823
  57.6 1.1 %update.1 = (f32[3,27,64]{2,1,0:T(8,128)}, f32[1,64]{1,0:T(1,128)}, f32[1,64]{1,0:T(1,128)}, f32[27,64,64]{2,1,0:T(8,128)}, f32[6,27,64]{2,1,0:T(8,128)}, /*index=5*/f32[1,1]{1,0:T(1,128)}) custom-call(bf16[16,40,128]{2,1,0:T(8,128)(2,1)S(1)} %all_to_all.16.mine_ref, bf16[16,40,128]{2,1,0:T(8,128)(2,1)S(1)} %collective-permute-done.4.theirs_ref, ...), custom_call_target="tpu_custom_call" | custom-call | tf_op jit(solution)/shard_map/update/pallas_call | solution.py:807
  (1 shorter events, 0.0 us)
Async XLA Ops:
  2.2 7.4 %collective-permute-start = (f32[3,16,512]{2,1,0:T(8,128)S(1)}, f32[3,16,512]{2,1,0:T(8,128)S(1)}, u32[]{:S(2)}, u32[]{:S(2)}) collective-permute-start(f32[3,16,512]{2,1,0:T(8,128)S(1)} %get-tuple-element.36.near_ref), channel_id=1, source_target_pairs={{0,2},{2,0},{4,6},{6,4},{8,10},{10,8},{12,14},{14,12},{16,18},{18,... | collective-permute-start | bytes 294920 | tf_op jit(solution)/shard_map/ppermute | solution.py:838
  5.2 4.3 %collective-permute-start.1 = (f32[3,16,512]{2,1,0:T(8,128)S(1)}, f32[3,16,512]{2,1,0:T(8,128)S(1)}, u32[]{:S(2)}, u32[]{:S(2)}) collective-permute-start(f32[3,16,512]{2,1,0:T(8,128)S(1)} %get-tuple-element.37.far_ref), channel_id=1, source_target_pairs={{2,4},{4,2},{6,8},{8,6},{10,12},{12,10},{14,16},{16,14},{18,20},{2... | collective-permute-start | bytes 294920 | tf_op jit(solution)/shard_map/ppermute | solution.py:839
  5.9 3.7 %collective-permute-start.2 = (f32[3,16,512]{2,1,0:T(8,128)S(1)}, f32[3,16,512]{2,1,0:T(8,128)S(1)}, u32[]{:S(2)}, u32[]{:S(2)}) collective-permute-start(f32[3,16,512]{2,1,0:T(8,128)S(1)} %get-tuple-element.38.plane_ref), channel_id=1, source_target_pairs={{0,1},{1,0},{2,3},{3,2},{4,5},{5,4},{6,7},{7,6},{8,9},{9,8},{10,11... | collective-permute-start | bytes 294920 | tf_op jit(solution)/shard_map/ppermute | solution.py:823
  6.0 3.2 %copy-start = (f32[27,64,64]{2,1,0:T(8,128)S(1)}, f32[27,64,64]{2,1,0:T(8,128)}, u32[]{:S(2)}) copy-start(f32[27,64,64]{2,1,0:T(8,128)} %wm_ref.3) | copy-start | bytes 1327108
  6.0 3.1 %copy-start.1 = (f32[27,6,64]{2,0,1:T(8,128)S(1)}, f32[27,6,64]{2,0,1:T(8,128)}, u32[]{:S(2)}) copy-start(f32[27,6,64]{2,0,1:T(8,128)} %param.19) | copy-start | bytes 124420
  6.0 3.1 %copy-start.2 = (f32[27,64,3]{1,0,2:T(8,128)S(1)}, f32[27,64,3]{1,0,2:T(8,128)}, u32[]{:S(2)}) copy-start(f32[27,64,3]{1,0,2:T(8,128)} %param.15) | copy-start | bytes 62212
  8.5 2.4 %copy-start.5 = (f32[3,16,16,512]{3,2,1,0:T(8,128)}, f32[3,16,16,512]{3,2,1,0:T(8,128)S(1)}, u32[]{:S(2)}) copy-start(f32[3,16,16,512]{3,2,1,0:T(8,128)S(1)} %get-tuple-element.39.vn_ref) | copy-start | bytes 4718596
  10.9 16.5 %all-to-all-start = ((bf16[16,8,256]{2,1,0:T(8,128)(2,1)}), bf16[16,8,256]{2,1,0:T(8,128)(2,1)S(1)}, u32[]{:S(2)}, u32[]{:S(2)}) async-start(bf16[16,8,256]{2,1,0:T(8,128)(2,1)} %bitcast.5), calls=%async_computation | async-start | bytes 131072 | tf_op jit(solution)/shard_map/all_to_all | solution.py:847
  19.9 1.4 %copy-start.6 = (f32[3,16,16,512]{3,2,1,0:T(8,128)S(1)}, f32[3,16,16,512]{3,2,1,0:T(8,128)}, u32[]{:S(2)}) copy-start(f32[3,16,16,512]{3,2,1,0:T(8,128)} %copy-done.5) | copy-start | bytes 4718596
  21.3 6.1 %copy-start.3 = (f32[64]{0:T(128)S(1)}, f32[64]{0:T(128)}, u32[]{:S(2)}) copy-start(f32[64]{0:T(128)} %param.16) | copy-start | bytes 772
  21.3 6.1 %copy-start.4 = (f32[64]{0:T(128)S(1)}, f32[64]{0:T(128)}, u32[]{:S(2)}) copy-start(f32[64]{0:T(128)} %param.17) | copy-start | bytes 772
  32.5 1.5 %collective-permute-start.3 = (bf16[16,40,128]{2,1,0:T(8,128)(2,1)S(1)}, bf16[16,40,128]{2,1,0:T(8,128)(2,1)S(1)}, u32[]{:S(2)}, u32[]{:S(2)}) collective-permute-start(bf16[16,40,128]{2,1,0:T(8,128)(2,1)S(1)} %get-tuple-element.48), channel_id=1, source_target_pairs={{0,1},{1,0},{2,3},{3,2},{4,5},{5,4},{6,7},{7,6},{8,9},{9,8},{10,11... | collective-permute-start | bytes 491528 | tf_op jit(solution)/shard_map/ppermute | solution.py:823
  56.2 1.4 %collective-permute-start.4 = (bf16[16,40,128]{2,1,0:T(8,128)(2,1)S(1)}, bf16[16,40,128]{2,1,0:T(8,128)(2,1)S(1)}, u32[]{:S(2)}, u32[]{:S(2)}) collective-permute-start(bf16[16,40,128]{2,1,0:T(8,128)(2,1)S(1)} %all_to_all.16.mine_ref), channel_id=1, source_target_pairs={{0,1},{1,0},{2,3},{3,2},{4,5},{5,4},{6,7},{7,6},{8,9},{9,8},{10,11... | collective-permute-start | bytes 491528 | tf_op jit(solution)/shard_map/ppermute | solution.py:823
